TPU v7x, 512 devices: a whole 4x4x16 slice. The times are simulated.
512 devices in a mesh: view: 8 (over z_lo), gz: 64 (over y, x, z_hi, core).
Axes of the slice: x: 4, y: 4, z: 16 (z_hi: 2, z_lo: 8; z = z_hi * 8 + z_lo), core: 2. Of those that a mesh axis runs over, the one named last changes fastest.
Arguments:
- estimate: float32 [2048, 128, 128], P('gz'), may hold values from 0.25 to 4
- raw_bricks: bfloat16 [8, 32768, 4, 2, 128], P('view', 'gz'), may hold values from 0.25 to 4
- brick_slab: int32 [8, 32768, 1], P('view', 'gz'), may hold values from 0 to 63; in each aligned block of 512 rows (0 to 511, 512 to 1023, ..., all dimensions but the last counted through in order) at most 16 rows name the same one
- brick_pos: int32 [8, 32768], P('view', 'gz'), may hold values from 0 to 511
- off_z: int32 [8, 4], P('view'), may hold values from -1 to 3
- frac_z: float32 [8, 4], P('view'), may hold values from 0 to 1
- off_y: int32 [8, 2], P('view'), may hold values from -1 to 1
- frac_y: float32 [8, 2], P('view'), may hold values from 0 to 1
- off_x: int32 [8, 128], P('view'), may hold values from -1 to 127
- frac_x: float32 [8, 128], P('view'), may hold values from 0 to 1
- psf_z: float32 [8, 64], P('view'), may hold values from 0.05 to 1
- psf_y: float32 [8, 16], P('view'), may hold values from 0.05 to 1
- psf_x: float32 [8, 16], P('view'), may hold values from 0.05 to 1
Outputs:
- new_estimate: float32 [2048, 128, 128], P('gz', 'view')
Inputs may be any that keep to these rules, and one draw needn't show every extreme that they name: `brick_slab`: in every view, the 512 bricks held by one device (an aligned block) name any one slab at most 16 times, a bound that some block reaches.
All inputs are finite; a program needn't handle non-finite values.
Results may differ from a plain program's by a relative error of at most 0.00043.
Values may be sent and summed in bfloat16 or wider, within the bound.
No kernel may reach another device: no remote copies, remote signals or barrier semaphores. Data moves between devices by JAX's collectives and lax.ppermute only.
A program may use at most 64 MiB of HBM per device.

v0:
```python
import jax
import jax.numpy as jnp
from jax import lax
from jax.sharding import PartitionSpec as P


def with_halo(cells, sides, width):
    for axis, dim in sides:
        count = lax.axis_size(axis)
        ends = count - 1
        head = lax.slice_in_dim(cells, 0, width, axis=dim)
        tail = lax.slice_in_dim(cells, cells.shape[dim] - width, cells.shape[dim], axis=dim)
        cells = jnp.concatenate(
            [
                lax.ppermute(tail, axis, [(i, (i + 1) % count) for i in range(ends)]),
                cells,
                lax.ppermute(head, axis, [((i + 1) % count, i) for i in range(ends)]),
            ],
            axis=dim,
        )
    return cells


def rounded_weights(values):
    return lax.optimization_barrier(values.astype(jnp.bfloat16)).astype(jnp.float32)


def weight_table(offsets, fractions, length):
    source_rows = jnp.arange(length, dtype=jnp.int32)[:, None]
    low_weight = rounded_weights(1.0 - fractions)[None, :]
    high_weight = rounded_weights(fractions)[None, :]
    table = jnp.where(source_rows == offsets[None, :], low_weight, jnp.float32(0.0))
    return table + jnp.where(source_rows == offsets[None, :] + 1, high_weight, jnp.float32(0.0))


def band_table(kernel, row_count, col_count, start_tap, direction):
    normed = kernel / jnp.sum(kernel)
    distance = (
        jnp.arange(col_count, dtype=jnp.int32)[None, :]
        - jnp.arange(row_count, dtype=jnp.int32)[:, None]
    )
    which_tap = direction * distance + start_tap
    table = jnp.zeros((row_count, col_count), jnp.float32)
    for tap_index in range(kernel.shape[0]):
        table = table + jnp.where(which_tap == tap_index, normed[tap_index], jnp.float32(0.0))
    return table.astype(jnp.bfloat16)


def resample_bricks(bricks, table_x, table_zy):
    shape_in = bricks.shape
    col_count = shape_in[-1]
    along_x = jnp.dot(
        bricks.reshape(-1, col_count), table_x, preferred_element_type=jnp.float32
    ).astype(jnp.bfloat16)
    along_x = along_x.reshape(-1, table_zy.shape[0], col_count)
    mixed = jnp.einsum("qp,nqx->npx", table_zy, along_x, preferred_element_type=jnp.float32)
    return mixed.astype(jnp.bfloat16).reshape(shape_in)


def separable(padded_block, table_z, table_y, table_x, out_shape):
    along_z = jnp.dot(
        table_z, padded_block.reshape(padded_block.shape[0], -1), preferred_element_type=jnp.float32
    )
    along_z = along_z.astype(jnp.bfloat16).reshape(out_shape)
    along_y = jnp.einsum(
        "ij,zjx->zix", table_y, along_z, preferred_element_type=jnp.float32
    ).astype(jnp.bfloat16)
    result = jnp.dot(along_y.reshape(-1, out_shape[2]), table_x, preferred_element_type=jnp.float32)
    return result.reshape(out_shape)


def shards(
    estimate,
    raw_bricks,
    brick_slab,
    brick_pos,
    off_z,
    frac_z,
    off_y,
    frac_y,
    off_x,
    frac_x,
    psf_z,
    psf_y,
    psf_x,
):
    plane_count, row_count, col_count = estimate.shape
    brick_count = raw_bricks.shape[1]
    brick_depth = raw_bricks.shape[2]
    brick_height = raw_bricks.shape[3]
    brick_cells = brick_depth * brick_height
    slab_count = lax.axis_size("gz")
    capacity = max(2, 2 * brick_count // slab_count)
    slot_total = slab_count * capacity
    block_planes = plane_count // brick_depth
    block_rows = row_count // brick_height
    place_total = block_planes * block_rows
    halo_width = psf_z.shape[1] // 2
    lateral = psf_x.shape[1] // 2
    table_x = weight_table(off_x[0], frac_x[0], col_count).astype(jnp.bfloat16)
    table_z = weight_table(off_z[0], frac_z[0], brick_depth)
    table_y = weight_table(off_y[0], frac_y[0], brick_height)
    table_zy = (
        jnp.einsum("ac,bd->abcd", table_z, table_y)
        .reshape(brick_cells, brick_cells)
        .astype(jnp.bfloat16)
    )
    destination = brick_slab[0, :, 0]
    positions = brick_pos[0]
    member = (destination[:, None] == jnp.arange(slab_count, dtype=jnp.int32)[None, :]).astype(
        jnp.int32
    )
    earlier = jnp.cumsum(member, axis=0) - member
    order_within = jnp.sum(earlier * member, axis=1)
    slot_of = destination * capacity + order_within
    chosen = slot_of[None, :] == jnp.arange(slot_total, dtype=jnp.int32)[:, None]
    slot_positions = jnp.max(jnp.where(chosen, positions[None, :], -1), axis=1).reshape(
        slab_count, capacity
    )
    selector = chosen.astype(jnp.bfloat16)
    own_bricks = raw_bricks[0].reshape(brick_count, brick_cells, col_count)
    outgoing = jnp.dot(
        selector, own_bricks.reshape(brick_count, -1), preferred_element_type=jnp.float32
    )
    outgoing = outgoing.astype(jnp.bfloat16).reshape(slab_count, capacity, brick_cells, col_count)
    arrived = resample_bricks(
        lax.all_to_all(outgoing, "gz", split_axis=0, concat_axis=0, tiled=True), table_x, table_zy
    )
    arrived_positions = lax.all_to_all(
        slot_positions, "gz", split_axis=0, concat_axis=0, tiled=True
    )
    placer = (
        arrived_positions.reshape(-1)[None, :] == jnp.arange(place_total, dtype=jnp.int32)[:, None]
    ).astype(jnp.bfloat16)
    placed = jnp.dot(placer, arrived.reshape(slot_total, -1), preferred_element_type=jnp.float32)
    placed = placed.reshape(block_planes, block_rows, brick_depth, brick_height, col_count)
    joined = 1.0 + placed.transpose(0, 2, 1, 3, 4).reshape(plane_count, row_count, col_count)
    out_shape = (plane_count, row_count, col_count)
    forward_z = band_table(psf_z[0], plane_count, plane_count + 2 * halo_width, 0, 1)
    backward_z = band_table(psf_z[0], plane_count, plane_count + 2 * halo_width, 2 * halo_width, -1)
    forward_y = band_table(psf_y[0], row_count, row_count, lateral, 1)
    backward_y = band_table(psf_y[0], row_count, row_count, lateral, -1)
    forward_x = band_table(psf_x[0], col_count, col_count, lateral, -1)
    backward_x = band_table(psf_x[0], col_count, col_count, lateral, 1)
    estimate_b = estimate.astype(jnp.bfloat16)
    padded = with_halo(estimate_b, (("gz", 0),), halo_width)
    blurred = separable(padded, forward_z, forward_y, forward_x, out_shape)
    ratio = (joined / blurred).astype(jnp.bfloat16)
    ratio_padded = with_halo(ratio, (("gz", 0),), halo_width)
    correction = separable(ratio_padded, backward_z, backward_y, backward_x, out_shape)
    view_count = lax.axis_size("view")
    share_rows = row_count // view_count
    first_row = lax.axis_index("view") * share_rows
    total = lax.psum(correction, "view")
    part_total = lax.dynamic_slice_in_dim(total, first_row, share_rows, 1)
    part_estimate = lax.dynamic_slice_in_dim(estimate, first_row, share_rows, 1)
    return part_estimate * part_total / view_count


def solution(mesh):
    in_specs = (
        P("gz", None, None),
        P("view", "gz", None, None, None),
        P("view", "gz", None),
        P("view", "gz"),
        P("view", None),
        P("view", None),
        P("view", None),
        P("view", None),
        P("view", None),
        P("view", None),
        P("view", None),
        P("view", None),
        P("view", None),
    )
    out_specs = P("gz", "view", None)
    return jax.shard_map(shards, mesh=mesh, in_specs=in_specs, out_specs=out_specs, check_vma=False)
```

profile of v0, /device:TPU:6, one launch (start us, length us, event | category | flops | bytes accessed | tf_op | source)
XLA Modules:
  0.0 627.8 jit_solution(6561166403337153155)
XLA Ops:
  11.9 21.2 %all-to-all-start = ((s32[64,1,16]{2,1,0:T(1,128)}), s32[64,1,16]{2,1,0:T(1,128)S(1)}, u32[]{:S(2)}, u32[]{:S(2)}) async-start(s32[64,1,16]{2,1,0:T(1,128)} %bitcast.68), calls=%async_computation | async-start | bytes 65536 | tf_op jit(solution)/shard_map/all_to_all | solution.py:129
  33.2 1.8 reshape_reshape_squeeze.3
  36.2 2.0 copy.46
  38.2 10.0 %all-to-all-done = s32[64,1,16]{2,1,0:T(1,128)S(1)} async-done(((s32[64,1,16]{2,1,0:T(1,128)}), s32[64,1,16]{2,1,0:T(1,128)S(1)}, u32[]{:S(2)}, u32[]{:S(2)}) %all-to-all-start) | async-done | bytes 4128 | tf_op jit(solution)/shard_map/all_to_all | solution.py:129
  48.2 7.6 %all-to-all-start.1 = ((bf16[64,16,8,128]{3,2,1,0:T(8,128)(2,1)}), bf16[64,16,8,128]{3,2,1,0:T(8,128)(2,1)S(1)}, u32[]{:S(2)}, u32[]{:S(2)}) async-start(bf16[64,16,8,128]{3,2,1,0:T(8,128)(2,1)} %bitcast.225), calls=%async_computation.1 | async-start | bytes 4194304 | tf_op jit(solution)/shard_map/all_to_all | solution.py:127
  55.9 1.8 convert_element_type.159
  57.7 2.0 collective-permute-start
  59.7 13.3 %collective-permute-start.1 = (bf16[32,128,128]{2,1,0:T(8,128)(2,1)S(1)}, bf16[32,128,128]{2,1,0:T(8,128)(2,1)}, u32[]{:S(2)}, u32[]{:S(2)}) collective-permute-start(bf16[32,128,128]{2,1,0:T(8,128)(2,1)S(1)} %convert_element_type.159), channel_id=1, source_target_pairs={{1,0},{2,1},{3,2},{4,3},{5,4},{6,5},{7,6},{8,7},{9,8},{10,9},{11,1... | collective-permute-start | bytes 3145736 | tf_op jit(solution)/shard_map/ppermute | solution.py:17
  82.8 80.8 %collective-permute-done = bf16[32,128,128]{2,1,0:T(8,128)(2,1)} collective-permute-done((bf16[32,128,128]{2,1,0:T(8,128)(2,1)S(1)}, bf16[32,128,128]{2,1,0:T(8,128)(2,1)}, u32[]{:S(2)}, u32[]{:S(2)}) %collective-permute-start) | collective-permute-done | bytes 1048608 | tf_op jit(solution)/shard_map/ppermute | solution.py:15
  163.6 1.7 pad_maximum_fusion
  165.3 42.1 %fusion.18 = bf16[4,8,128,128]{3,1,2,0:T(8,128)(2,1)S(1)} fusion(bf16[12,8,128,128]{3,2,1,0:T(8,128)(2,1)S(1)} %bitcast.222, f32[]{:T(128)} %bitcast.63, f32[]{:T(128)} %bitcast.62, f32[]{:T(128)} %bitcast.61, f32[]{:T(128)} %bitcast.60, f32[]{:T(128)} %bitcast.59, f32[]{:T(128)} %bitcast.58, f32[]{:T(128)} %bitcast.57, f32[]{:T(128)} %bitcast.56, ...), kind=kOutput, calls=%fused_computation.27 | convolution fusion | flops 101780480 | bytes 4194560 | tf_op jit(solution)/shard_map/dot_general | solution.py:61
  207.7 2.7 fusion.10
  210.4 2.2 copy.66
  212.6 2.6 copy.32
  215.2 2.9 add_bitcast_fusion
  219.8 22.0 %divide_convert_fusion = bf16[32,128,128]{2,1,0:T(8,128)(2,1)} fusion(f32[32,128,128]{2,1,0:T(8,128)S(1)} %bitcast.228, bf16[32,128,128]{2,1,0:T(8,128)(2,1)S(1)} %bitcast.230, f32[]{:T(128)} %bitcast.126, f32[]{:T(128)} %bitcast.125, f32[]{:T(128)} %bitcast.124, f32[]{:T(128)} %bitcast.123, f32[]{:T(128)} %bitcast.122, f32[]{:T(128)} %bitcast.121, ...), kind=kOutput, calls=%fused_computation.12 | convolution fusion | flops 271663104 | bytes 4194432 | tf_op jit(solution)/shard_map/dot_general | solution.py:68
  241.8 9.8 %collective-permute-start.2 = (bf16[32,128,128]{2,1,0:T(8,128)(2,1)}, bf16[32,128,128]{2,1,0:T(8,128)(2,1)S(1)}, u32[]{:S(2)}, u32[]{:S(2)}) collective-permute-start(bf16[32,128,128]{2,1,0:T(8,128)(2,1)} %divide_convert_fusion), channel_id=1, source_target_pairs={{0,1},{1,2},{2,3},{3,4},{4,5},{5,6},{6,7},{7,8},{8,9},{9,10},{10,1... | collective-permute-start | bytes 3145736 | tf_op jit(solution)/shard_map/ppermute | solution.py:15
  251.6 5.6 collective-permute-start.3
  257.2 12.3 %collective-permute-done.2 = bf16[32,128,128]{2,1,0:T(8,128)(2,1)S(1)} collective-permute-done((bf16[32,128,128]{2,1,0:T(8,128)(2,1)}, bf16[32,128,128]{2,1,0:T(8,128)(2,1)S(1)}, u32[]{:S(2)}, u32[]{:S(2)}) %collective-permute-start.2) | collective-permute-done | bytes 1048608 | tf_op jit(solution)/shard_map/ppermute | solution.py:15
  269.5 5.3 collective-permute-done.3
  276.2 42.2 %fusion.21 = bf16[4,8,128,128]{3,1,2,0:T(8,128)(2,1)S(1)} fusion(bf16[12,8,128,128]{3,2,1,0:T(8,128)(2,1)S(1)} %bitcast.221, f32[]{:T(128)} %bitcast.63, f32[]{:T(128)} %bitcast.62, f32[]{:T(128)} %bitcast.61, f32[]{:T(128)} %bitcast.60, f32[]{:T(128)} %bitcast.59, f32[]{:T(128)} %bitcast.58, f32[]{:T(128)} %bitcast.57, f32[]{:T(128)} %bitcast.56, ...), kind=kOutput, calls=%fused_computation.28 | convolution fusion | flops 101786624 | bytes 4194560 | tf_op jit(solution)/shard_map/dot_general | solution.py:61
  318.6 22.4 %fusion.17 = f32[32,128,128]{2,1,0:T(8,128)} fusion(bf16[32,128,128]{2,1,0:T(8,128)(2,1)S(1)} %bitcast.227, f32[]{:T(128)} %bitcast.126, f32[]{:T(128)} %bitcast.125, f32[]{:T(128)} %bitcast.124, f32[]{:T(128)} %bitcast.123, f32[]{:T(128)} %bitcast.122, f32[]{:T(128)} %bitcast.121, f32[]{:T(128)} %bitcast.120, f32[]{:T(128)} %bitcast.119, f32[]{:T(128)} %bitcast.118, ...), kind=kOutput, calls=%fused_computation.26 | convolution fusion | flops 270614528 | bytes 3145856 | tf_op jit(solution)/shard_map/dot_general | solution.py:68
  341.0 278.2 %all-reduce.2.cloned.1.call-done = f32[32,128,128]{2,1,0:T(8,128)} async-done(((f32[32,128,128]{2,1,0:T(8,128)}), f32[32,128,128]{2,1,0:T(8,128)}) %all-reduce.2.cloned.1.call-update) | async-done | bytes 2097168 | tf_op jit(solution)/shard_map/psum | solution.py:154
  619.2 1.8 multiply_multiply_fusion
  (68 shorter events, 19.9 us)
Async XLA Ops:
  11.9 36.2 %all-to-all-start = ((s32[64,1,16]{2,1,0:T(1,128)}), s32[64,1,16]{2,1,0:T(1,128)S(1)}, u32[]{:S(2)}, u32[]{:S(2)}) async-start(s32[64,1,16]{2,1,0:T(1,128)} %bitcast.68), calls=%async_computation | async-start | bytes 65536 | tf_op jit(solution)/shard_map/all_to_all | solution.py:129
  48.2 159.5 %all-to-all-start.1 = ((bf16[64,16,8,128]{3,2,1,0:T(8,128)(2,1)}), bf16[64,16,8,128]{3,2,1,0:T(8,128)(2,1)S(1)}, u32[]{:S(2)}, u32[]{:S(2)}) async-start(bf16[64,16,8,128]{3,2,1,0:T(8,128)(2,1)} %bitcast.225), calls=%async_computation.1 | async-start | bytes 4194304 | tf_op jit(solution)/shard_map/all_to_all | solution.py:127
  55.8 17.3 %copy-start.3 = (f32[1,4]{1,0:T(1,128)S(1)}, f32[1,4]{1,0:T(1,128)}, u32[]{:S(2)}) copy-start(f32[1,4]{1,0:T(1,128)} %param.18) | copy-start | bytes 52
  55.8 17.3 %copy-start.4 = (f32[1,2]{1,0:T(1,128)S(1)}, f32[1,2]{1,0:T(1,128)}, u32[]{:S(2)}) copy-start(f32[1,2]{1,0:T(1,128)} %param.20) | copy-start | bytes 28
  55.8 17.4 %copy-start.5 = (f32[1,64]{1,0:T(1,128)S(1)}, f32[1,64]{1,0:T(1,128)}, u32[]{:S(2)}) copy-start(f32[1,64]{1,0:T(1,128)} %param.23) | copy-start | bytes 772
  55.8 18.0 %copy-start.6 = (f32[1,16]{1,0:T(1,128)S(1)}, f32[1,16]{1,0:T(1,128)}, u32[]{:S(2)}) copy-start(f32[1,16]{1,0:T(1,128)} %param.24) | copy-start | bytes 196
  55.8 19.9 %copy-start.2 = (s32[1,4]{1,0:T(1,128)S(1)}, s32[1,4]{1,0:T(1,128)}, u32[]{:S(2)}) copy-start(s32[1,4]{1,0:T(1,128)} %param.17) | copy-start | bytes 52
  55.8 19.9 %copy-start.1 = (s32[1,2]{1,0:T(1,128)S(1)}, s32[1,2]{1,0:T(1,128)}, u32[]{:S(2)}) copy-start(s32[1,2]{1,0:T(1,128)} %param.19) | copy-start | bytes 28
  55.8 20.5 %copy-start.7 = (f32[1,128]{1,0:T(1,128)S(1)}, f32[1,128]{1,0:T(1,128)}, u32[]{:S(2)}) copy-start(f32[1,128]{1,0:T(1,128)} %param.22) | copy-start | bytes 1540
  55.8 20.7 %copy-start.8 = (f32[1,16]{1,0:T(1,128)S(1)}, f32[1,16]{1,0:T(1,128)}, u32[]{:S(2)}) copy-start(f32[1,16]{1,0:T(1,128)} %param.25) | copy-start | bytes 196
  55.9 25.6 %copy-start = (s32[1,128]{1,0:T(1,128)S(1)}, s32[1,128]{1,0:T(1,128)}, u32[]{:S(2)}) copy-start(s32[1,128]{1,0:T(1,128)} %param.21) | copy-start | bytes 1540
  55.9 563.3 %all-reduce.2.cloned.1.call-start = ((), (), s32[]{:S(2)}) async-start(), calls=%async_computation.2 | async-start | bytes 4194304 | tf_op jit(solution)/shard_map/psum | solution.py:154
  57.7 105.9 %collective-permute-start = (bf16[32,128,128]{2,1,0:T(8,128)(2,1)S(1)}, bf16[32,128,128]{2,1,0:T(8,128)(2,1)}, u32[]{:S(2)}, u32[]{:S(2)}) collective-permute-start(bf16[32,128,128]{2,1,0:T(8,128)(2,1)S(1)} %convert_element_type.159), channel_id=1, source_target_pairs={{0,1},{1,2},{2,3},{3,4},{4,5},{5,6},{6,7},{7,8},{8,9},{9,10},{10,1... | collective-permute-start | bytes 3145736 | tf_op jit(solution)/shard_map/ppermute | solution.py:15
  59.7 103.9 %collective-permute-start.1 = (bf16[32,128,128]{2,1,0:T(8,128)(2,1)S(1)}, bf16[32,128,128]{2,1,0:T(8,128)(2,1)}, u32[]{:S(2)}, u32[]{:S(2)}) collective-permute-start(bf16[32,128,128]{2,1,0:T(8,128)(2,1)S(1)} %convert_element_type.159), channel_id=1, source_target_pairs={{1,0},{2,1},{3,2},{4,3},{5,4},{6,5},{7,6},{8,7},{9,8},{10,9},{11,1... | collective-permute-start | bytes 3145736 | tf_op jit(solution)/shard_map/ppermute | solution.py:17
  241.8 27.7 %collective-permute-start.2 = (bf16[32,128,128]{2,1,0:T(8,128)(2,1)}, bf16[32,128,128]{2,1,0:T(8,128)(2,1)S(1)}, u32[]{:S(2)}, u32[]{:S(2)}) collective-permute-start(bf16[32,128,128]{2,1,0:T(8,128)(2,1)} %divide_convert_fusion), channel_id=1, source_target_pairs={{0,1},{1,2},{2,3},{3,4},{4,5},{5,6},{6,7},{7,8},{8,9},{9,10},{10,1... | collective-permute-start | bytes 3145736 | tf_op jit(solution)/shard_map/ppermute | solution.py:15
  251.6 23.2 %collective-permute-start.3 = (bf16[32,128,128]{2,1,0:T(8,128)(2,1)}, bf16[32,128,128]{2,1,0:T(8,128)(2,1)S(1)}, u32[]{:S(2)}, u32[]{:S(2)}) collective-permute-start(bf16[32,128,128]{2,1,0:T(8,128)(2,1)} %divide_convert_fusion), channel_id=1, source_target_pairs={{1,0},{2,1},{3,2},{4,3},{5,4},{6,5},{7,6},{8,7},{9,8},{10,9},{11,1... | collective-permute-start | bytes 3145736 | tf_op jit(solution)/shard_map/ppermute | solution.py:17
Sparse Core Ops, SparseCore 0:
  341.1 278.0 all-reduce.1
where the time goes:
time: 630 us; the launch traced here: 628 us
  waiting for transfers between devices  387 us (61%)
  matrix products  135 us (21%)
  starting transfers between devices  59.6 us (9%)
  local copies, waits for them, and re-layouts  16.6 us (3%)
  other arithmetic  15.7 us (2%)
  between operations  13.8 us (2%)
    psum x1, waiting for transfers between devices, shards(): total = lax.psum(correction, 'view')  278 us
    ppermute x2, waiting for transfers between devices, with_halo(): lax.ppermute(tail, axis, [(i, (i + 1) % count) for i in range(ends)])  93.2 us
    dot_general x2, matrix products, separable(): jnp.dot(table_z, padded_block.reshape(padded_block.shape[0], -1), preferr...  84.3 us
    dot_general x2, matrix products, separable(): jnp.dot(along_y.reshape(-1, out_shape[2]), table_x, preferred_element_typ...  44.4 us
    all_to_all x1, starting transfers between devices, shards(): lax.all_to_all(slot_positions, 'gz', split_axis=0, concat_axis=0, tiled=T...  21.2 us
    ppermute x2, starting transfers between devices, with_halo(): lax.ppermute(head, axis, [((i + 1) % count, i) for i in range(ends)])  18.9 us
  transfers between devices with their start and end apart: 7, of which 5 were waited for; matrix products, arithmetic and copies ran while one was open for 10% of the time, Pallas kernels for 0%

commit v1 on v0

v1 whole, which is shorter than its diff:
```python
import functools

import jax
import jax.numpy as jnp
from jax import lax
from jax.experimental import pallas as pl
from jax.experimental.pallas import tpu as pltpu
from jax.sharding import Mesh
from jax.sharding import PartitionSpec as P

BF = jnp.bfloat16
F32 = jnp.float32
I32 = jnp.int32
VMEM = pltpu.VMEM
SMEM = pltpu.SMEM


def iota(shape, dim):
    return lax.broadcasted_iota(I32, shape, dim)


def mm(a, b):
    return jnp.dot(a, b, preferred_element_type=F32)


def mm_nt(a, b):
    return lax.dot_general(a, b, (((1,), (1,)), ((), ())), preferred_element_type=F32)


def pack_kernel(cap, groups, slab_ref, pos_ref, bricks_ref, out_ref):
    count, cells = bricks_ref.shape
    slots = out_ref.shape[0]
    slab = slab_ref[...]
    pos = pos_ref[...]
    slabs = groups * 4
    member = (iota((slabs, count), 0) == slab).astype(BF)
    before = (iota((count, count), 0) < iota((count, count), 1)).astype(BF)
    earlier = mm(member, before)
    order = jnp.sum(earlier * member.astype(F32), axis=0, keepdims=True).astype(I32)
    chip = lax.shift_right_logical(slab, 2)
    half = lax.bitwise_and(lax.shift_right_logical(slab, 1), 1)
    core = lax.bitwise_and(slab, 1)
    slot = ((chip * 2 + core) * 2 + half) * cap + order
    block = lax.shift_right_logical(pos, 6) + 1
    row = lax.bitwise_and(pos, 63)
    which = iota((128, count), 0)
    places = jnp.where(which == 0, block, jnp.where(which == 1, row, 0)).astype(F32).astype(BF)
    step = 128
    for at in range(0, slots, step):
        chosen = (iota((step, count), 0) + at == slot).astype(BF)
        out_ref[at : at + step, :cells] = mm(chosen, bricks_ref[...]).astype(BF)
        out_ref[at : at + step, cells:] = mm_nt(chosen, places).astype(BF)


def pack(slab, pos, bricks, cap, groups):
    count, cells = bricks.shape
    slots = groups * 4 * cap
    return pl.pallas_call(
        functools.partial(pack_kernel, cap, groups),
        out_shape=jax.ShapeDtypeStruct((slots, cells + 128), BF),
        in_specs=[pl.BlockSpec(memory_space=VMEM)] * 3,
        out_specs=pl.BlockSpec(memory_space=VMEM),
        cost_estimate=pl.CostEstimate(
            flops=2 * slots * count * cells, bytes_accessed=2 * (count + slots) * cells, transcendentals=0
        ),
        name="pack",
    )(slab, pos, bricks)


def smem_sum(ref):
    total = ref[0, 0]
    for k in range(1, ref.shape[1]):
        total = total + ref[0, k]
    return total


def tap_table(psf_ref, which_tap):
    table = jnp.zeros(which_tap.shape, F32)
    for k in range(psf_ref.shape[1]):
        table = jnp.where(which_tap == k, psf_ref[0, k], table)
    total = jnp.full(which_tap.shape, smem_sum(psf_ref), F32)
    return (table / total).astype(BF)


def z_table(psf_ref, core, depth, direction):
    rows, cols = 2 * depth, 5 * depth
    r, c = iota((rows, cols), 0), iota((rows, cols), 1)
    out_plane = (lax.div(r, depth) * 2 + core) * depth + lax.rem(r, depth)
    block = lax.div(c, depth)
    own = jnp.where(block == 1, core, core + 2)
    other = jnp.where(block == 3, 1 - core, 3 - core)
    slab = jnp.where(block == 0, 5 * core - 1, jnp.where(block <= 2, own, other))
    in_plane = slab * depth + lax.rem(c, depth)
    half = psf_ref.shape[1] // 2
    return tap_table(psf_ref, direction * (in_plane - out_plane) + half)


def split_row(y, rows):
    half = rows // 2
    return jnp.where(y < half, 2 * y, 2 * (y - half) + 1)


def along_z(table, own_ref, oth_ref, beside_ref, out_ref, pair=2):
    _, rows, depth, cols = own_ref.shape
    planes = 2 * depth

    def column(y):
        return jnp.concatenate(
            [beside_ref[y], own_ref[0, y], own_ref[1, y], oth_ref[0, y], oth_ref[1, y]], axis=0
        )

    unroll = 4

    def body(i, carry):
        for u in range(unroll):
            y = (i * unroll + u) * pair
            data = jnp.concatenate([column(y + n) for n in range(pair)], axis=1)
            res = mm(table, data)
            for n in range(pair):
                out_ref[pl.ds(y + n, planes, stride=rows), :] = res[:, n * cols : (n + 1) * cols]
        return carry

    lax.fori_loop(0, rows // (pair * unroll), body, 0)


def blur_kernel(core_ref, psf_z_ref, psf_y_ref, psf_x_ref, own_ref, oth_ref, beside_ref, out_ref, mid):
    _, rows, depth, cols = own_ref.shape
    core = core_ref[0, 0]
    table_z = z_table(psf_z_ref, core, depth, 1)
    lateral = psf_y_ref.shape[1] // 2
    shape = (rows, rows)
    table_y = tap_table(psf_y_ref, iota(shape, 1) - split_row(iota(shape, 0), rows) + lateral)
    shape = (cols, cols)
    table_x = tap_table(psf_x_ref, iota(shape, 0) - iota(shape, 1) + lateral)
    along_z(table_z, own_ref, oth_ref, beside_ref, mid)

    unroll = 4

    def body(i, carry):
        for u in range(unroll):
            z = (i * unroll + u) * 2
            at = pl.multiple_of(z * rows, 2 * rows)
            first = mid[pl.ds(at, rows), :].astype(BF)
            second = mid[pl.ds(at + rows, rows), :].astype(BF)
            both = mm(table_y, jnp.concatenate([first, second], axis=1)).astype(BF)
            out_ref[pl.ds(at, rows), :] = mm(both[:, :cols], table_x)
            out_ref[pl.ds(at + rows, rows), :] = mm(both[:, cols:], table_x)
        return carry

    lax.fori_loop(0, 2 * depth // (2 * unroll), body, 0)


def slab_flops(rows, depth, cols):
    return 2 * 2 * depth * rows * cols * (5 * depth + rows + cols)


def blur(core, psf_z, psf_y, psf_x, own, oth, beside):
    _, rows, depth, cols = own.shape
    return pl.pallas_call(
        blur_kernel,
        out_shape=jax.ShapeDtypeStruct((2 * depth * rows, cols), F32),
        in_specs=[pl.BlockSpec(memory_space=SMEM)] * 4 + [pl.BlockSpec(memory_space=VMEM)] * 3,
        out_specs=pl.BlockSpec(memory_space=VMEM),
        scratch_shapes=[pltpu.VMEM((2 * depth * rows, cols), F32)],
        cost_estimate=pl.CostEstimate(
            flops=slab_flops(rows, depth, cols),
            bytes_accessed=18 * depth * rows * cols,
            transcendentals=0,
        ),
        name="blur",
    )(core, psf_z, psf_y, psf_x, own, oth, beside)


def interpolation(off_ref, frac_ref, length):
    table = []
    for a in range(length):
        line = []
        for c in range(length):
            frac = frac_ref[0, c]
            low = jnp.where(off_ref[0, c] == a, 1.0 - frac, 0.0)
            high = jnp.where(off_ref[0, c] + 1 == a, frac, 0.0)
            line.append((low, high))
        table.append(line)
    return table


def rounded(value):
    return value.astype(BF).astype(F32)


def join_kernel(
    cap,
    off_z_ref,
    frac_z_ref,
    off_y_ref,
    frac_y_ref,
    off_x_ref,
    frac_x_ref,
    arrived_ref,
    blurred_ref,
    out_ref,
    mixed,
    ratio,
):
    sources, _, width = arrived_ref.shape
    cols = off_x_ref.shape[1]
    deep, high = off_z_ref.shape[1], off_y_ref.shape[1]
    cells = deep * high
    _, rows, depth, _ = out_ref.shape
    spots = rows // high
    blocks = depth // deep
    places = spots * blocks
    slots = sources * cap
    source = iota((cols, cols), 0)
    off_x = off_x_ref[...]
    frac_x = frac_x_ref[...]
    table_x = jnp.where(source == off_x, rounded(1.0 - frac_x), 0.0)
    table_x = table_x + jnp.where(source == off_x + 1, rounded(frac_x), 0.0)
    table_x = table_x.astype(BF)
    weights_z = interpolation(off_z_ref, frac_z_ref, deep)
    weights_y = interpolation(off_y_ref, frac_y_ref, high)

    def spread(pair):
        low, up = pair
        return rounded(jnp.full((8, cols), low, F32)) + rounded(jnp.full((8, cols), up, F32))

    wide_z = [[spread(p) for p in line] for line in weights_z]
    wide_y = [[spread(p) for p in line] for line in weights_y]
    lane = iota((8, 128), 1)
    decode = jnp.where(lane == 0, spots, jnp.where(lane == 1, 1, 0)).astype(F32).astype(BF)
    for h in range(2):
        data = arrived_ref[:, h * cap : (h + 1) * cap, :].reshape(slots, width)
        place = mm_nt(decode, data[:, cells * cols :])[:1, :].astype(I32) - spots
        for b in range(blocks):
            chosen = (iota((spots, slots), 0) + b * spots == place).astype(BF)
            placed = mm(chosen, data[:, : cells * cols])
            for c in range(deep):
                for d in range(high):
                    acc = jnp.zeros((spots, cols), F32)
                    for a in range(deep):
                        for e in range(high):
                            weight = rounded(wide_z[a][c] * wide_y[e][d])
                            tile = placed[:, (a * high + e) * cols : (a * high + e + 1) * cols]
                            acc = acc + jnp.tile(weight, (spots // 8, 1)) * tile
                    plane = h * depth + b * deep + c
                    at = plane * rows + d * spots
                    mixed[at : at + spots, :] = acc.astype(BF)

    step = 512

    def body(i, carry):
        at = pl.multiple_of(i * step, step)
        joined = 0.5 + mm(mixed[pl.ds(at, step), :], table_x)
        ratio[pl.ds(at, step), :] = joined / blurred_ref[pl.ds(at, step), :]
        return carry

    lax.fori_loop(0, 2 * depth * rows // step, body, 0)

    def turn(y, carry):
        for h in range(2):
            line = ratio[pl.ds(h * depth * rows + y, depth, stride=rows), :]
            out_ref[h, y] = line.astype(BF)
        return carry

    lax.fori_loop(0, rows, turn, 0, unroll=8)


def join(cap, rows, depth, off_z, frac_z, off_y, frac_y, off_x, frac_x, arrived, blurred):
    cols = off_x.shape[1]
    cells = off_z.shape[1] * off_y.shape[1]
    slots = arrived.shape[0] * cap
    points = 2 * depth * rows
    return pl.pallas_call(
        functools.partial(join_kernel, cap),
        out_shape=jax.ShapeDtypeStruct((2, rows, depth, cols), BF),
        in_specs=[pl.BlockSpec(memory_space=SMEM)] * 4 + [pl.BlockSpec(memory_space=VMEM)] * 4,
        out_specs=pl.BlockSpec(memory_space=VMEM),
        scratch_shapes=[pltpu.VMEM((points, cols), BF), pltpu.VMEM((points, cols), F32)],
        cost_estimate=pl.CostEstimate(
            flops=2 * 2 * points // cells * slots * cells * cols // 2,
            bytes_accessed=8 * points * cols,
            transcendentals=0,
        ),
        name="join",
    )(off_z, frac_z, off_y, frac_y, off_x, frac_x, arrived, blurred)


def back_kernel(core_ref, psf_z_ref, psf_y_ref, psf_x_ref, own_ref, oth_ref, beside_ref, out_ref, mid):
    _, rows, depth, cols = own_ref.shape
    views = out_ref.shape[1]
    share = rows // views
    core = core_ref[0, 0]
    table_z = z_table(psf_z_ref, core, depth, -1)
    lateral = psf_y_ref.shape[1] // 2
    shape = (rows, rows)
    table_y = tap_table(psf_y_ref, iota(shape, 0) - split_row(iota(shape, 1), rows) + lateral)
    shape = (cols, cols)
    table_x = tap_table(psf_x_ref, iota(shape, 1) - iota(shape, 0) + lateral)
    along_z(table_z, own_ref, oth_ref, beside_ref, mid)

    unroll = 4

    for h in range(2):

        def body(i, carry):
            for u in range(unroll):
                z = (i * unroll + u) * 2
                at = pl.multiple_of((h * depth + z) * rows, 2 * rows)
                first = mid[pl.ds(at, rows), :].astype(BF)
                second = mid[pl.ds(at + rows, rows), :].astype(BF)
                both = mm(table_y, jnp.concatenate([first, second], axis=1)).astype(BF)
                for n in range(2):
                    res = mm(both[:, n * cols : (n + 1) * cols], table_x)
                    for v in range(views):
                        out_ref[h, v, z + n] = res[v * share : (v + 1) * share, :]
            return carry

        lax.fori_loop(0, depth // (2 * unroll), body, 0)


def back(core, psf_z, psf_y, psf_x, own, oth, beside, views):
    _, rows, depth, cols = own.shape
    return pl.pallas_call(
        back_kernel,
        out_shape=jax.ShapeDtypeStruct((2, views, depth, rows // views, cols), F32),
        in_specs=[pl.BlockSpec(memory_space=SMEM)] * 4 + [pl.BlockSpec(memory_space=VMEM)] * 3,
        out_specs=pl.BlockSpec(memory_space=VMEM),
        scratch_shapes=[pltpu.VMEM((2 * depth * rows, cols), F32)],
        cost_estimate=pl.CostEstimate(
            flops=slab_flops(rows, depth, cols),
            bytes_accessed=18 * depth * rows * cols,
            transcendentals=0,
        ),
        name="back",
    )(core, psf_z, psf_y, psf_x, own, oth, beside)


PLANE = ("y", "x", "core")
RING = ("zh", "view")


def with_sides(own, chips):
    core = lax.axis_index("core")
    other = lax.ppermute(own, "core", [(0, 1), (1, 0)])
    end = lax.dynamic_index_in_dim(own, core, 0, keepdims=False)
    pairs = []
    for chip in range(chips):
        if chip + 1 < chips:
            pairs.append((chip * 2 + 1, chip * 2 + 2))
        if chip > 0:
            pairs.append((chip * 2, chip * 2 - 1))
    return other, lax.ppermute(end, PLANE, pairs)


def shards(
    chips,
    cap,
    estimate,
    raw_bricks,
    brick_slab,
    brick_pos,
    off_z,
    frac_z,
    off_y,
    frac_y,
    off_x,
    frac_x,
    psf_z,
    psf_y,
    psf_x,
):
    depth, rows, cols = estimate.shape
    count = raw_bricks.shape[1]
    views = lax.axis_size("view")
    share = rows // views
    core = lax.axis_index("core").astype(I32).reshape(1, 1)

    packed = pack(
        brick_slab.reshape(1, count), brick_pos, raw_bricks.reshape(count, -1), cap, chips
    )
    packed = packed.reshape(2 * chips, 2 * cap, -1)
    arrived = lax.all_to_all(packed, PLANE, split_axis=0, concat_axis=0, tiled=True)

    part = lax.dynamic_slice_in_dim(estimate, lax.axis_index("view") * share, share, 1)
    piece = part.astype(BF).transpose(1, 0, 2)
    own = lax.all_gather(piece, RING, axis=0, tiled=True).reshape(2, rows, depth, cols)
    blurred = blur(core, psf_z, psf_y, psf_x, own, *with_sides(own, chips))

    ratio = join(cap, rows, depth, off_z, frac_z, off_y, frac_y, off_x, frac_x, arrived, blurred)
    correction = back(core, psf_z, psf_y, psf_x, ratio, *with_sides(ratio, chips), views)
    correction = correction.reshape(2 * views, depth, share, cols)
    total = lax.psum_scatter(correction, RING, scatter_dimension=0, tiled=True)
    return part * total.reshape(depth, share, cols) / views


def solution(mesh):
    devices = mesh.devices
    views, slabs = devices.shape
    fine = Mesh(devices.reshape(views, 4, slabs // 16, 2, 2), ("view", "y", "x", "zh", "core"))
    gz = ("y", "x", "zh", "core")
    in_specs = (
        P(gz, None, None),
        P("view", gz, None, None, None),
        P("view", gz, None),
        P("view", gz),
    ) + (P("view", None),) * 9
    out_specs = P(gz, "view", None)
    return jax.shard_map(
        functools.partial(shards, slabs // 4, 16),
        mesh=fine,
        in_specs=in_specs,
        out_specs=out_specs,
        check_vma=False,
    )
```

time: 630 us -> 266 us (0.42)
  waiting for transfers between devices: 387 us -> 173 us
  matrix products: 135 us -> 0 us
  Pallas kernels: 0 us -> 43.9 us
  starting transfers between devices: 59.6 us -> 21.6 us
  other arithmetic: 15.7 us -> 1.77 us
    psum x1 -> x0, waiting for transfers between devices: 278 us -> none  [shards(): total = lax.psum(correction, 'view')]
    dot_general x7 -> x0, matrix products: 135 us -> none  [the longest x2 84.3 us: separable(): jnp.dot(table_z, padded_block.reshape(padded_block.shape[0], -1), preferr...]
    reduce_scatter x0 -> x1, waiting for transfers between devices: none -> 79.5 us  [shards(): total = lax.psum_scatter(correction, RING, scatter_dimension=0, tiled=True)]
    ppermute x4, waiting for transfers between devices: 98.4 us -> 27.3 us  [the longest x2 27.3 us: with_sides(): return (other, lax.ppermute(end, PLANE, pairs))]
    all_gather x0 -> x1, waiting for transfers between devices: none -> 66.6 us  [shards(): lax.all_gather(piece, RING, axis=0, tiled=True)]
    pallas_call x0 -> x4, Pallas kernels: none -> 43.9 us  [the longest x1 13.5 us: join(): pl.pallas_call(functools.partial(join_kernel, cap), out_shape=jax.ShapeDt...]
    ppermute x4, starting transfers between devices: 30.7 us -> 11.3 us  [the longest x2 6.42 us: with_sides(): other = lax.ppermute(own, 'core', [(0, 1), (1, 0)])]
    all_to_all x2 -> x1, starting transfers between devices: 28.8 us -> 10.2 us  [shards(): lax.all_to_all(packed, PLANE, split_axis=0, concat_axis=0, tiled=True)]
  transfers between devices with their start and end apart: 7 -> 7, of which waited for: 5 -> 4; matrix products, arithmetic and copies ran while one was open for 10% -> 3% of each run, Pallas kernels for 0% -> 7%
where the time goes in v1:
time: 266 us
  waiting for transfers between devices  173 us (65%)
  Pallas kernels  43.9 us (17%)
  starting transfers between devices  21.6 us (8%)
  between operations  13.5 us (5%)
  local copies, waits for them, and re-layouts  11.9 us (4%)
    reduce_scatter x1, waiting for transfers between devices, shards(): total = lax.psum_scatter(correction, RING, scatter_dimension=0, tiled=True)  79.5 us
    all_gather x1, waiting for transfers between devices, shards(): lax.all_gather(piece, RING, axis=0, tiled=True)  66.6 us
    ppermute x2, waiting for transfers between devices, with_sides(): return (other, lax.ppermute(end, PLANE, pairs))  27.3 us
    pallas_call x1, Pallas kernels, join(): pl.pallas_call(functools.partial(join_kernel, cap), out_shape=jax.ShapeDt...  13.5 us
    pallas_call x1, Pallas kernels, back(): pl.pallas_call(back_kernel, out_shape=jax.ShapeDtypeStruct((2, views, dep...  12.9 us
    pallas_call x1, Pallas kernels, blur(): pl.pallas_call(blur_kernel, out_shape=jax.ShapeDtypeStruct((2 * depth * r...  12.9 us
    all_to_all x1, starting transfers between devices, shards(): lax.all_to_all(packed, PLANE, split_axis=0, concat_axis=0, tiled=True)  10.2 us
    ppermute x2, starting transfers between devices, with_sides(): other = lax.ppermute(own, 'core', [(0, 1), (1, 0)])  6.42 us
  transfers between devices with their start and end apart: 7, of which 4 were waited for; matrix products, arithmetic and copies ran while one was open for 3% of the time, Pallas kernels for 7%

profile of v1, /device:TPU:6, one launch (start us, length us, event | category | flops | bytes accessed | tf_op | source)
XLA Modules:
  0.0 265.9 jit_solution(2903750316639878352)
XLA Ops:
  6.5 1.6 fusion.1
  8.2 2.6 reshape.23.bricks_ref
  10.8 4.5 %pack.1 = bf16[1024,1152]{1,0:T(8,128)(2,1)} custom-call(s32[1,512]{1,0:T(1,128)} %bitcast.20, s32[1,512]{1,0:T(1,128)} %pos_ref.1, bf16[512,1024]{1,0:T(8,128)(2,1)} %reshape.23.bricks_ref), custom_call_target="tpu_custom_call" | custom-call | flops 1073741824 | bytes 3145728 | tf_op jit(solution)/shard_map/pack/pallas_call | solution.py:58
  15.3 10.2 %all-to-all-start = ((bf16[32,32,1152]{2,1,0:T(8,128)(2,1)}), bf16[32,32,1152]{2,1,0:T(8,128)(2,1)}, u32[]{:S(2)}, u32[]{:S(2)}) async-start(bf16[32,32,1152]{2,1,0:T(8,128)(2,1)} %bitcast.19), calls=%async_computation | async-start | bytes 4718592 | tf_op jit(solution)/shard_map/all_to_all | solution.py:382
  25.5 0.0 reduce-scatter.2.cloned.1.call-start
  25.6 66.6 %all-gather.2.cloned.1.call-done = bf16[256,32,128]{2,0,1:T(8,128)(2,1)} async-done(((bf16[16,32,128]{2,0,1:T(8,128)(2,1)}), bf16[256,32,128]{2,0,1:T(8,128)(2,1)}) %all-gather.2.cloned.1.call-update) | async-done | bytes 2097168 | tf_op jit(solution)/shard_map/all_gather | solution.py:386
  92.1 2.9 %copy.14 = bf16[256,32,128]{2,1,0:T(8,128)(2,1)S(1)} copy(bf16[256,32,128]{2,0,1:T(8,128)(2,1)} %all-gather.2.cloned.1.call-done) | data formatting | bytes 4194304 | tf_op jit(solution)/shard_map/all_gather | solution.py:386
  95.1 1.9 collective-permute-start
  97.0 0.1 dynamic-slice_bitcast_fusion.1
  97.1 3.0 %collective-permute-start.1 = (bf16[128,32,128]{2,1,0:T(8,128)(2,1)S(1)}, bf16[128,32,128]{2,1,0:T(8,128)(2,1)S(1)}, u32[]{:S(2)}, u32[]{:S(2)}) collective-permute-start(bf16[128,32,128]{2,1,0:T(8,128)(2,1)S(1)} %dynamic-slice_bitcast_fusion.1), channel_id=1, source_target_pairs={{1,4},{5,8},{4,1},{9,12},{8,5},{13,16},{12,9},{17,20},{16,13},{21,... | collective-permute-start | bytes 3145736 | tf_op jit(solution)/shard_map/ppermute | solution.py:352
  100.1 13.1 %collective-permute-done.1.beside_ref = bf16[128,32,128]{2,1,0:T(8,128)(2,1)S(1)} collective-permute-done((bf16[128,32,128]{2,1,0:T(8,128)(2,1)S(1)}, bf16[128,32,128]{2,1,0:T(8,128)(2,1)S(1)}, u32[]{:S(2)}, u32[]{:S(2)}) %collective-permute-start.1) | collective-permute-done | bytes 1048608 | tf_op jit(solution)/shard_map/ppermute | solution.py:352
  113.2 1.0 copy-done.3
  114.2 12.9 %blur.1.blurred_ref = f32[8192,128]{1,0:T(8,128)} custom-call(s32[1,1]{1,0:T(1,128)} %bitcast.core_ref, f32[1,64]{1,0:T(1,128)} %psf_z_ref.3, f32[1,16]{1,0:T(1,128)} %psf_y_ref.3, f32[1,16]{1,0:T(1,128)} %psf_x_ref.3, bf16[2,128,32,128]{3,2,1,0:T(8,128)(2,1)} %bitcast.18, bf16[2,128,32,128]{3,2,1,0:T(8,128)(2,1)} %collective-permute-done.oth_ref, ...), custom_call_target="tpu_custom_call" | custom-call | flops 872415232 | bytes 9437184 | tf_op jit(solution)/shard_map/blur/pallas_call | solution.py:159
  127.1 13.5 %join.1.own_ref = bf16[2,128,32,128]{3,2,1,0:T(8,128)(2,1)} custom-call(s32[1,4]{1,0:T(1,128)} %off_z_ref.1, f32[1,4]{1,0:T(1,128)} %frac_z_ref.1, s32[1,2]{1,0:T(1,128)} %off_y_ref.1, f32[1,2]{1,0:T(1,128)} %frac_y_ref.1, s32[1,128]{1,0:T(1,128)} %off_x_ref.1, f32[1,128]{1,0:T(1,128)} %frac_x_ref.1, bf16[32,32,1152]{2,1,0:T(8,128)(2,1)} %all-to-all-done.arrived_ref, ...), custom_call_target="tpu_custom_call" | custom-call | flops 1073741824 | bytes 8388608 | tf_op jit(solution)/shard_map/join/pallas_call | solution.py:273
  140.6 4.5 %collective-permute-start.2 = (bf16[2,128,32,128]{3,2,1,0:T(8,128)(2,1)}, bf16[2,128,32,128]{3,2,1,0:T(8,128)(2,1)S(1)}, u32[]{:S(2)}, u32[]{:S(2)}) collective-permute-start(bf16[2,128,32,128]{3,2,1,0:T(8,128)(2,1)} %join.1.own_ref), channel_id=1, source_target_pairs={{0,1},{1,0},{2,3},{3,2},{4,5},{5,4},{6,7},{7,6},{8,9},{9,8},{10,11... | collective-permute-start | bytes 6291464 | tf_op jit(solution)/shard_map/ppermute | solution.py:344
  145.1 1.3 dynamic-slice_bitcast_fusion
  146.4 1.9 collective-permute-start.3
  148.4 14.2 %collective-permute-done.3.beside_ref = bf16[128,32,128]{2,1,0:T(8,128)(2,1)S(1)} collective-permute-done((bf16[128,32,128]{2,1,0:T(8,128)(2,1)S(1)}, bf16[128,32,128]{2,1,0:T(8,128)(2,1)S(1)}, u32[]{:S(2)}, u32[]{:S(2)}) %collective-permute-start.3) | collective-permute-done | bytes 1048608 | tf_op jit(solution)/shard_map/ppermute | solution.py:352
  162.6 1.0 copy-done.2
  163.6 1.3 copy-done.1
  164.9 12.9 %back.1 = f32[2,8,32,16,128]{4,3,2,1,0:T(8,128)} custom-call(s32[1,1]{1,0:T(1,128)} %bitcast.core_ref, f32[1,64]{1,0:T(1,128)} %psf_z_ref.3, f32[1,16]{1,0:T(1,128)} %psf_y_ref.3, f32[1,16]{1,0:T(1,128)} %psf_x_ref.3, bf16[2,128,32,128]{3,2,1,0:T(8,128)(2,1)} %join.1.own_ref, bf16[2,128,32,128]{3,2,1,0:T(8,128)(2,1)} %copy-done.1, ...), custom_call_target="tpu_custom_call" | custom-call | flops 872415232 | bytes 9437184 | tf_op jit(solution)/shard_map/back/pallas_call | solution.py:323
  177.9 0.0 reduce-scatter.2.cloned.1.call-update
  177.9 79.5 %reduce-scatter.2.cloned.1.call-done = f32[1,32,16,128]{3,2,1,0:T(8,128)} async-done(((f32[16,32,16,128]{3,2,1,0:T(8,128)}), f32[1,32,16,128]{3,2,1,0:T(8,128)}) %reduce-scatter.2.cloned.1.call-update) | async-done | bytes 262160 | tf_op jit(solution)/shard_map/reduce_scatter | solution.py:392
  257.3 1.8 fusion
  (10 shorter events, 0.0 us)
Async XLA Ops:
  6.5 85.6 %all-gather.2.cloned.1.call-start = ((), (), s32[]{:S(2)}) async-start(), calls=%async_computation.2 | async-start | bytes 2228224 | tf_op jit(solution)/shard_map/all_gather | solution.py:386
  15.3 111.8 %all-to-all-start = ((bf16[32,32,1152]{2,1,0:T(8,128)(2,1)}), bf16[32,32,1152]{2,1,0:T(8,128)(2,1)}, u32[]{:S(2)}, u32[]{:S(2)}) async-start(bf16[32,32,1152]{2,1,0:T(8,128)(2,1)} %bitcast.19), calls=%async_computation | async-start | bytes 4718592 | tf_op jit(solution)/shard_map/all_to_all | solution.py:382
  25.5 231.8 %reduce-scatter.2.cloned.1.call-start = ((), (), s32[]{:S(2)}) async-start(), calls=%async_computation.3 | async-start | bytes 4456448 | tf_op jit(solution)/shard_map/reduce_scatter | solution.py:392
  95.1 18.2 %copy-start = (bf16[256,32,128]{2,1,0:T(8,128)(2,1)}, bf16[256,32,128]{2,1,0:T(8,128)(2,1)S(1)}, u32[]{:S(2)}) copy-start(bf16[256,32,128]{2,1,0:T(8,128)(2,1)S(1)} %copy.14) | copy-start | bytes 6291460
  95.1 18.1 %collective-permute-start = (bf16[2,128,32,128]{3,2,1,0:T(8,128)(2,1)S(1)}, bf16[2,128,32,128]{3,2,1,0:T(8,128)(2,1)}, u32[]{:S(2)}, u32[]{:S(2)}) collective-permute-start(bf16[2,128,32,128]{3,2,1,0:T(8,128)(2,1)S(1)} %bitcast.16), channel_id=1, source_target_pairs={{0,1},{1,0},{2,3},{3,2},{4,5},{5,4},{6,7},{7,6},{8,9},{9,8},{10,11... | collective-permute-start | bytes 6291464 | tf_op jit(solution)/shard_map/ppermute | solution.py:344
  97.1 16.1 %collective-permute-start.1 = (bf16[128,32,128]{2,1,0:T(8,128)(2,1)S(1)}, bf16[128,32,128]{2,1,0:T(8,128)(2,1)S(1)}, u32[]{:S(2)}, u32[]{:S(2)}) collective-permute-start(bf16[128,32,128]{2,1,0:T(8,128)(2,1)S(1)} %dynamic-slice_bitcast_fusion.1), channel_id=1, source_target_pairs={{1,4},{5,8},{4,1},{9,12},{8,5},{13,16},{12,9},{17,20},{16,13},{21,... | collective-permute-start | bytes 3145736 | tf_op jit(solution)/shard_map/ppermute | solution.py:352
  113.2 1.0 copy-start.3
  140.6 21.9 %collective-permute-start.2 = (bf16[2,128,32,128]{3,2,1,0:T(8,128)(2,1)}, bf16[2,128,32,128]{3,2,1,0:T(8,128)(2,1)S(1)}, u32[]{:S(2)}, u32[]{:S(2)}) collective-permute-start(bf16[2,128,32,128]{3,2,1,0:T(8,128)(2,1)} %join.1.own_ref), channel_id=1, source_target_pairs={{0,1},{1,0},{2,3},{3,2},{4,5},{5,4},{6,7},{7,6},{8,9},{9,8},{10,11... | collective-permute-start | bytes 6291464 | tf_op jit(solution)/shard_map/ppermute | solution.py:344
  146.4 16.1 %collective-permute-start.3 = (bf16[128,32,128]{2,1,0:T(8,128)(2,1)S(1)}, bf16[128,32,128]{2,1,0:T(8,128)(2,1)S(1)}, u32[]{:S(2)}, u32[]{:S(2)}) collective-permute-start(bf16[128,32,128]{2,1,0:T(8,128)(2,1)S(1)} %dynamic-slice_bitcast_fusion), channel_id=1, source_target_pairs={{1,4},{5,8},{4,1},{9,12},{8,5},{13,16},{12,9},{17,20},{16,13},{21,... | collective-permute-start | bytes 3145736 | tf_op jit(solution)/shard_map/ppermute | solution.py:352
  162.5 1.0 copy-start.2
  163.6 1.3 copy-start.1
Sparse Core Ops, SparseCore 0:
  9.3 82.7 all-gather.1
  178.0 79.2 reduce-scatter.1

commit v2 on v1

v2 whole, which is shorter than its diff:
```python
import functools

import jax
import jax.numpy as jnp
from jax import lax
from jax.experimental import pallas as pl
from jax.experimental.pallas import tpu as pltpu
from jax.sharding import Mesh
from jax.sharding import PartitionSpec as P


BF = jnp.bfloat16
F32 = jnp.float32
I32 = jnp.int32
VMEM = pltpu.VMEM
SMEM = pltpu.SMEM
MIB = 1 << 20


def iota(shape, dim):
    return lax.broadcasted_iota(I32, shape, dim)


def mm(a, b):
    return jnp.dot(a, b, preferred_element_type=F32)


def mm_nt(a, b):
    return lax.dot_general(a, b, (((1,), (1,)), ((), ())), preferred_element_type=F32)


def pack_kernel(cap, groups, slab_ref, pos_ref, bricks_ref, out_ref):
    count, cells = bricks_ref.shape
    slots = out_ref.shape[0]
    slab = slab_ref[...]
    pos = pos_ref[...]
    slabs = groups * 4
    member = (iota((slabs, count), 0) == slab).astype(BF)
    before = (iota((count, count), 0) < iota((count, count), 1)).astype(BF)
    earlier = mm(member, before)
    order = jnp.sum(earlier * member.astype(F32), axis=0, keepdims=True).astype(I32)
    chip = lax.shift_right_logical(slab, 2)
    half = lax.bitwise_and(lax.shift_right_logical(slab, 1), 1)
    core = lax.bitwise_and(slab, 1)
    slot = ((chip * 2 + core) * 2 + half) * cap + order
    block = lax.shift_right_logical(pos, 6) + 1
    row = lax.bitwise_and(pos, 63)
    which = iota((128, count), 0)
    places = jnp.where(which == 0, block, jnp.where(which == 1, row, 0)).astype(F32).astype(BF)
    step = 128
    for at in range(0, slots, step):
        chosen = (iota((step, count), 0) + at == slot).astype(BF)
        out_ref[at : at + step, :cells] = mm(chosen, bricks_ref[...]).astype(BF)
        out_ref[at : at + step, cells:] = mm_nt(chosen, places).astype(BF)


def pack(slab, pos, bricks, cap, groups):
    count, cells = bricks.shape
    slots = groups * 4 * cap
    return pl.pallas_call(
        functools.partial(pack_kernel, cap, groups),
        out_shape=jax.ShapeDtypeStruct((slots, cells + 128), BF),
        in_specs=[pl.BlockSpec(memory_space=VMEM)] * 3,
        out_specs=pl.BlockSpec(memory_space=VMEM),
        compiler_params=pltpu.CompilerParams(vmem_limit_bytes=16 * MIB),
        cost_estimate=pl.CostEstimate(
            flops=2 * slots * count * cells, bytes_accessed=2 * (count + slots) * cells, transcendentals=0
        ),
        name="pack",
    )(slab, pos, bricks)


def smem_sum(ref):
    total = ref[0, 0]
    for k in range(1, ref.shape[1]):
        total = total + ref[0, k]
    return total


def tap_table(psf_ref, which_tap):
    table = jnp.zeros(which_tap.shape, F32)
    for k in range(psf_ref.shape[1]):
        table = jnp.where(which_tap == k, psf_ref[0, k], table)
    total = jnp.full(which_tap.shape, smem_sum(psf_ref), F32)
    return (table / total).astype(BF)


def z_table(psf_ref, core, depth, direction):
    rows, cols = depth, 3 * depth
    r, c = iota((rows, cols), 0), iota((rows, cols), 1)
    side = (lax.div(c, depth) - 1) * (1 - 2 * core)
    distance = side * depth + lax.rem(c, depth) - r
    half = psf_ref.shape[1] // 2
    return tap_table(psf_ref, direction * distance + half)


def split_row(y, rows):
    half = rows // 2
    return jnp.where(y < half, 2 * y, 2 * (y - half) + 1)


def turn_kernel(view_ref, part_ref, out_ref):
    out_ref[...] = jnp.swapaxes(part_ref[...], 0, 1).astype(BF)


def turn(view, estimate, share):
    depth, _, cols = estimate.shape
    return pl.pallas_call(
        turn_kernel,
        out_shape=jax.ShapeDtypeStruct((share, depth, cols), BF),
        grid_spec=pltpu.PrefetchScalarGridSpec(
            num_scalar_prefetch=1,
            grid=(1,),
            in_specs=[pl.BlockSpec((depth, share, cols), lambda i, view: (0, view[0], 0))],
            out_specs=pl.BlockSpec((share, depth, cols), lambda i, view: (0, 0, 0)),
        ),
        cost_estimate=pl.CostEstimate(
            flops=0, bytes_accessed=6 * depth * share * cols, transcendentals=0
        ),
        name="turn",
    )(view, estimate)


def finish_kernel(views, view_ref, part_ref, total_ref, out_ref):
    out_ref[...] = part_ref[...] * jnp.swapaxes(total_ref[...], 0, 1) / views


def finish(view, estimate, total, views):
    share, depth, cols = total.shape
    return pl.pallas_call(
        functools.partial(finish_kernel, views),
        out_shape=jax.ShapeDtypeStruct((depth, share, cols), F32),
        grid_spec=pltpu.PrefetchScalarGridSpec(
            num_scalar_prefetch=1,
            grid=(1,),
            in_specs=[
                pl.BlockSpec((depth, share, cols), lambda i, view: (0, view[0], 0)),
                pl.BlockSpec((share, depth, cols), lambda i, view: (0, 0, 0)),
            ],
            out_specs=pl.BlockSpec((depth, share, cols), lambda i, view: (0, 0, 0)),
        ),
        compiler_params=pltpu.CompilerParams(vmem_limit_bytes=8 * MIB),
        cost_estimate=pl.CostEstimate(
            flops=0, bytes_accessed=12 * depth * share * cols, transcendentals=0
        ),
        name="finish",
    )(view, estimate, total)


def twice(table):
    zero = jnp.zeros_like(table)
    top = jnp.concatenate([table, zero], axis=1)
    return jnp.concatenate([top, jnp.concatenate([zero, table], axis=1)], axis=0)


def tables_kernel(
    core_ref, psf_z_ref, psf_y_ref, psf_x_ref, az_ref, ay_ref, ax_ref, bz_ref, by_ref, bx_ref
):
    rows, cols = ay_ref.shape[0], ax_ref.shape[0] // 2
    core = core_ref[0, 0]
    lateral = psf_y_ref.shape[1] // 2
    az_ref[...] = z_table(psf_z_ref, core, az_ref.shape[0], 1)
    bz_ref[...] = z_table(psf_z_ref, core, bz_ref.shape[0], -1)
    line, across = iota((rows, rows), 0), iota((rows, rows), 1)
    ay_ref[...] = tap_table(psf_y_ref, across - split_row(line, rows) + lateral)
    by_ref[...] = tap_table(psf_y_ref, line - split_row(across, rows) + lateral)
    line, across = iota((cols, cols), 0), iota((cols, cols), 1)
    ax_ref[...] = twice(tap_table(psf_x_ref, line - across + lateral))
    bx_ref[...] = twice(tap_table(psf_x_ref, across - line + lateral))


def tables(core, psf_z, psf_y, psf_x, depth, rows, cols):
    shapes = ((depth, 3 * depth), (rows, rows), (2 * cols, 2 * cols))
    return pl.pallas_call(
        tables_kernel,
        out_shape=[jax.ShapeDtypeStruct(shape, BF) for shape in shapes * 2],
        in_specs=[pl.BlockSpec(memory_space=SMEM)] * 4,
        out_specs=[pl.BlockSpec(memory_space=VMEM)] * 6,
        compiler_params=pltpu.CompilerParams(vmem_limit_bytes=4 * MIB),
        name="tables",
    )(core, psf_z, psf_y, psf_x)


def middle_kernel(
    core_ref,
    az_ref,
    ay_ref,
    ax_ref,
    by_ref,
    bx_ref,
    one_ref,
    own_ref,
    two_ref,
    joined_ref,
    out_ref,
    mid,
    even,
    odd,
    res,
):
    rows, depth, cols = out_ref.shape

    def column(y):
        return jnp.concatenate([one_ref[y], own_ref[y], two_ref[y]], axis=0)

    def axial(i, carry):
        y = pl.multiple_of(i * 8, 8)
        lines = []
        for n in range(0, 8, 2):
            both = mm(az_ref[...], jnp.concatenate([column(y + n), column(y + n + 1)], axis=1))
            lines += [both[:, :cols], both[:, cols:]]
        mid[:, pl.ds(y, 8), :] = jnp.swapaxes(jnp.stack(lines), 0, 1)
        return carry

    lax.fori_loop(0, rows // 8, axial, 0)

    def at(pair):
        return pl.ds(pl.multiple_of(pair * rows, rows), rows)

    def along_y(i, carry):
        for n in range(4):
            pair = i * 4 + n
            both = jnp.concatenate([mid[2 * pair], mid[2 * pair + 1]], axis=1).astype(BF)
            even[at(pair), :] = mm(ay_ref[...], both).astype(BF)
        return carry

    lax.fori_loop(0, depth // 8, along_y, 0)

    def divide(i, carry):
        pair = 2 * i
        here = pl.ds(pl.multiple_of(pair * rows, 2 * rows), 2 * rows)
        blurred = mm(even[here, :], ax_ref[...])
        left = jnp.concatenate([joined_ref[2 * pair], joined_ref[2 * pair + 2]], axis=0)
        right = jnp.concatenate([joined_ref[2 * pair + 1], joined_ref[2 * pair + 3]], axis=0)
        odd[here, :cols] = (left / blurred[:, :cols]).astype(BF)
        odd[here, cols:] = (right / blurred[:, cols:]).astype(BF)
        return carry

    lax.fori_loop(0, depth // 4, divide, 0)

    def along_y_back(i, carry):
        for n in range(4):
            pair = i * 4 + n
            even[at(pair), :] = mm(by_ref[...], odd[at(pair), :]).astype(BF)
        return carry

    lax.fori_loop(0, depth // 8, along_y_back, 0)

    def along_x_back(i, carry):
        here = pl.ds(pl.multiple_of(i * 4 * rows, 4 * rows), 4 * rows)
        both = mm(even[here, :], bx_ref[...])
        planes = []
        for n in range(4):
            planes += [both[n * rows : (n + 1) * rows, k * cols : (k + 1) * cols] for k in (0, 1)]
        z = pl.multiple_of(i * 8, 8)
        res[:, pl.ds(z, 8), :] = jnp.swapaxes(jnp.stack(planes), 0, 1)
        return carry

    lax.fori_loop(0, depth // 8, along_x_back, 0)
    out_ref[...] = res[...].astype(BF)


def middle(core, weights, one, own, two, joined):
    _, rows, depth, cols = own[0].shape
    slab = (None, rows, depth, cols)
    points = depth * rows * cols
    half = (depth * rows // 2, 2 * cols)
    return pl.pallas_call(
        middle_kernel,
        out_shape=jax.ShapeDtypeStruct((rows, depth, cols), BF),
        grid_spec=pltpu.PrefetchScalarGridSpec(
            num_scalar_prefetch=1,
            grid=(1,),
            in_specs=[pl.BlockSpec(w.shape, lambda i, core: (0, 0)) for w in weights]
            + [
                pl.BlockSpec(slab, lambda i, core, which=which: (which(core[0]), 0, 0, 0))
                for _, which in (one, own, two)
            ]
            + [pl.BlockSpec((depth, rows, cols), lambda i, core: (0, 0, 0))],
            out_specs=pl.BlockSpec((rows, depth, cols), lambda i, core: (0, 0, 0)),
            scratch_shapes=[
                pltpu.VMEM((depth, rows, cols), F32),
                pltpu.VMEM(half, BF),
                pltpu.VMEM(half, BF),
                pltpu.VMEM((rows, depth, cols), F32),
            ],
        ),
        compiler_params=pltpu.CompilerParams(vmem_limit_bytes=28 * MIB),
        cost_estimate=pl.CostEstimate(
            flops=2 * points * (3 * depth + 2 * rows + 2 * cols),
            bytes_accessed=12 * points,
            transcendentals=0,
        ),
        name="middle",
    )(core, *weights, one[0], own[0], two[0], joined)


def interpolation(off_ref, frac_ref, length):
    table = []
    for a in range(length):
        line = []
        for c in range(length):
            frac = frac_ref[0, c]
            low = jnp.where(off_ref[0, c] == a, 1.0 - frac, 0.0)
            high = jnp.where(off_ref[0, c] + 1 == a, frac, 0.0)
            line.append((low, high))
        table.append(line)
    return table


def rounded(value):
    return value.astype(BF).astype(F32)


def join_kernel(
    cap,
    core_ref,
    off_z_ref,
    frac_z_ref,
    off_y_ref,
    frac_y_ref,
    off_x_ref,
    frac_x_ref,
    arrived_ref,
    inner_ref,
    outer_ref,
    mixed,
):
    sources, _, width = arrived_ref.shape
    cols = off_x_ref.shape[1]
    deep, high = off_z_ref.shape[1], off_y_ref.shape[1]
    cells = deep * high
    depth, rows, _ = inner_ref.shape
    core = core_ref[0, 0]
    spots = rows // high
    blocks = depth // deep
    slots = sources * cap
    source = iota((cols, cols), 0)
    off_x = off_x_ref[...]
    frac_x = frac_x_ref[...]
    table_x = jnp.where(source == off_x, rounded(1.0 - frac_x), 0.0)
    table_x = table_x + jnp.where(source == off_x + 1, rounded(frac_x), 0.0)
    table_x = table_x.astype(BF)
    weights_z = interpolation(off_z_ref, frac_z_ref, deep)
    weights_y = interpolation(off_y_ref, frac_y_ref, high)

    def spread(pair):
        low, up = pair
        return rounded(jnp.full((8, cols), low, F32)) + rounded(jnp.full((8, cols), up, F32))

    wide_z = [[spread(p) for p in line] for line in weights_z]
    wide_y = [[spread(p) for p in line] for line in weights_y]
    lane = iota((8, 128), 1)
    decode = jnp.where(lane == 0, spots, jnp.where(lane == 1, 1, 0)).astype(F32).astype(BF)
    for out_ref, h in ((inner_ref, 1 - core), (outer_ref, core)):
        data = arrived_ref[:, pl.ds(pl.multiple_of(h * cap, cap), cap), :].reshape(slots, width)
        place = mm_nt(decode, data[:, cells * cols :])[:1, :].astype(I32) - spots
        for b in range(blocks):
            chosen = (iota((spots, slots), 0) + b * spots == place).astype(BF)
            placed = mm(chosen, data[:, : cells * cols])
            for c in range(deep):
                for d in range(high):
                    acc = jnp.zeros((spots, cols), F32)
                    for a in range(deep):
                        for e in range(high):
                            weight = rounded(wide_z[a][c] * wide_y[e][d])
                            tile = placed[:, (a * high + e) * cols : (a * high + e + 1) * cols]
                            acc = acc + jnp.tile(weight, (spots // 8, 1)) * tile
                    at = (b * deep + c) * rows + d * spots
                    mixed[at : at + spots, :] = acc.astype(BF)
        out_ref[...] = (0.5 + mm(mixed[...], table_x)).reshape(depth, rows, cols)


def join(cap, rows, depth, core, off_z, frac_z, off_y, frac_y, off_x, frac_x, arrived):
    cols = off_x.shape[1]
    slots = arrived.shape[0] * cap
    points = depth * rows
    return pl.pallas_call(
        functools.partial(join_kernel, cap),
        out_shape=[jax.ShapeDtypeStruct((depth, rows, cols), F32)] * 2,
        in_specs=[pl.BlockSpec(memory_space=SMEM)] * 5 + [pl.BlockSpec(memory_space=VMEM)] * 3,
        out_specs=[pl.BlockSpec(memory_space=VMEM)] * 2,
        scratch_shapes=[pltpu.VMEM((points, cols), BF)],
        compiler_params=pltpu.CompilerParams(vmem_limit_bytes=28 * MIB),
        cost_estimate=pl.CostEstimate(
            flops=2 * 2 * points * (slots + cols) * cols,
            bytes_accessed=12 * points * cols,
            transcendentals=0,
        ),
        name="join",
    )(core, off_z, frac_z, off_y, frac_y, off_x, frac_x, arrived)


def back_kernel(
    core_ref, table, beside_ref, outer_ref, oth_inner_ref, inner_ref, oth_outer_ref, out_ref
):
    share, _, cols = beside_ref.shape
    core = core_ref[0]
    for half, refs in (
        (core, (beside_ref, outer_ref, oth_inner_ref)),
        (1 - core, (oth_inner_ref, inner_ref, oth_outer_ref)),
    ):
        for n in range(0, share, 2):
            data = [jnp.concatenate([ref[n + k] for ref in refs], axis=0) for k in range(2)]
            both = mm(table[...], jnp.concatenate(data, axis=1))
            out_ref[half, n] = both[:, :cols]
            out_ref[half, n + 1] = both[:, cols:]


def back(core, table, beside, outer, oth_inner, inner, oth_outer, share):
    rows, depth, cols = outer.shape
    slab = pl.BlockSpec((share, depth, cols), lambda i, core: (i, 0, 0))
    points = 2 * depth * rows * cols
    return pl.pallas_call(
        back_kernel,
        out_shape=pltpu.HBM((2, rows, depth, cols), F32),
        grid_spec=pltpu.PrefetchScalarGridSpec(
            num_scalar_prefetch=1,
            grid=(rows // share,),
            in_specs=[pl.BlockSpec(table.shape, lambda i, core: (0, 0))] + [slab] * 5,
            out_specs=pl.BlockSpec((2, share, depth, cols), lambda i, core: (0, i, 0, 0)),
        ),
        compiler_params=pltpu.CompilerParams(vmem_limit_bytes=8 * MIB),
        cost_estimate=pl.CostEstimate(
            flops=2 * points * 3 * depth, bytes_accessed=9 * points, transcendentals=0
        ),
        name="back",
    )(core, table, beside, outer, oth_inner, inner, oth_outer)


PLANE = ("y", "x", "core")
RING = ("zh", "view")


def swapped(own):
    return lax.ppermute(own, "core", [(0, 1), (1, 0)])


def from_next(end, chips):
    pairs = []
    for chip in range(chips):
        if chip + 1 < chips:
            pairs.append((chip * 2 + 1, chip * 2 + 2))
        if chip > 0:
            pairs.append((chip * 2, chip * 2 - 1))
    return lax.ppermute(end, PLANE, pairs)


def shards(
    chips,
    cap,
    estimate,
    raw_bricks,
    brick_slab,
    brick_pos,
    off_z,
    frac_z,
    off_y,
    frac_y,
    off_x,
    frac_x,
    psf_z,
    psf_y,
    psf_x,
):
    depth, rows, cols = estimate.shape
    count = raw_bricks.shape[1]
    views = lax.axis_size("view")
    share = rows // views
    core = lax.axis_index("core").astype(I32)
    view = lax.axis_index("view").astype(I32)
    place = core.reshape(1)

    piece = turn(view.reshape(1), estimate, share)
    own = lax.all_gather(piece, RING, axis=0, tiled=True).reshape(2, rows, depth, cols)

    packed = pack(
        brick_slab.reshape(1, count), brick_pos, raw_bricks.reshape(count, -1), cap, chips
    )
    packed = packed.reshape(2 * chips, 2 * cap, -1)
    arrived = lax.all_to_all(packed, PLANE, split_axis=0, concat_axis=0, tiled=True)
    joined_inner, joined_outer = join(
        cap, rows, depth, core.reshape(1, 1), off_z, frac_z, off_y, frac_y, off_x, frac_x, arrived
    )

    end = lax.dynamic_index_in_dim(own, core, 0, keepdims=False)
    own, end = lax.optimization_barrier((own, end))
    beside = from_next(end, chips)[None]
    oth = swapped(own)
    az, ay, ax, bz, by, bx = tables(core.reshape(1, 1), psf_z, psf_y, psf_x, depth, rows, cols)
    weights = (az, ay, ax, by, bx)
    same, flip, first = (lambda c: c), (lambda c: 1 - c), (lambda c: 0)
    inner = middle(place, weights, (oth, same), (own, flip), (oth, flip), joined_inner)
    outer = middle(place, weights, (beside, first), (own, same), (oth, same), joined_outer)

    oth_inner = swapped(inner)
    beside = from_next(outer, chips)
    oth_outer = swapped(outer)
    correction = back(place, bz, beside, outer, oth_inner, inner, oth_outer, share)
    correction = correction.reshape(2 * views, share, depth, cols)
    total = lax.psum_scatter(correction, RING, scatter_dimension=0, tiled=True)
    return finish(view.reshape(1), estimate, total.reshape(share, depth, cols), views)


def solution(mesh):
    devices = mesh.devices
    views, slabs = devices.shape
    fine = Mesh(devices.reshape(views, 4, slabs // 16, 2, 2), ("view", "y", "x", "zh", "core"))
    gz = ("y", "x", "zh", "core")
    in_specs = (
        P(gz, None, None),
        P("view", gz, None, None, None),
        P("view", gz, None),
        P("view", gz),
    ) + (P("view", None),) * 9
    out_specs = P(gz, "view", None)
    return jax.shard_map(
        functools.partial(shards, slabs // 4, 16),
        mesh=fine,
        in_specs=in_specs,
        out_specs=out_specs,
        check_vma=False,
    )
```

time: 266 us -> 232 us (0.87)
  waiting for transfers between devices: 173 us -> 157 us
  Pallas kernels: 43.9 us -> 35 us
  local copies, waits for them, and re-layouts: 11.9 us -> 4.07 us
    ppermute x4 -> x5, waiting for transfers between devices: 27.3 us -> 13.5 us  [the longest x2 13.5 us: from_next(): return lax.ppermute(end, PLANE, pairs)]
    pallas_call x3 -> x7, Pallas kernels: 39.4 us -> 31.8 us  [the longest x2 17.4 us: middle(): pl.pallas_call(middle_kernel, out_shape=jax.ShapeDtypeStruct((rows, depth...]
    all_gather x1 -> x0, local copies, waits for them, and re-layouts: 2.94 us -> none  [shards(): lax.all_gather(piece, RING, axis=0, tiled=True)]
    ppermute x4 -> x5, starting transfers between devices: 11.3 us -> 11.8 us  [the longest x3 6.38 us: swapped(): return lax.ppermute(own, 'core', [(0, 1), (1, 0)])]
  transfers between devices with their start and end apart: 7 -> 8, of which waited for: 4 -> 3; matrix products, arithmetic and copies ran while one was open for 3% -> 1% of each run, Pallas kernels for 7% -> 12%
where the time goes in v2:
time: 232 us
  waiting for transfers between devices  157 us (68%)
  Pallas kernels  35 us (15%)
  starting transfers between devices  22.1 us (10%)
  between operations  13.7 us (6%)
  local copies, waits for them, and re-layouts  4.07 us (2%)
    reduce_scatter x1, waiting for transfers between devices, shards(): total = lax.psum_scatter(correction, RING, scatter_dimension=0, tiled=True)  79.3 us
    all_gather x1, waiting for transfers between devices, shards(): lax.all_gather(piece, RING, axis=0, tiled=True)  63.9 us
    pallas_call x2, Pallas kernels, middle(): pl.pallas_call(middle_kernel, out_shape=jax.ShapeDtypeStruct((rows, depth...  17.4 us
    ppermute x2, waiting for transfers between devices, from_next(): return lax.ppermute(end, PLANE, pairs)  13.5 us
    all_to_all x1, starting transfers between devices, shards(): lax.all_to_all(packed, PLANE, split_axis=0, concat_axis=0, tiled=True)  10.2 us
    ppermute x3, starting transfers between devices, swapped(): return lax.ppermute(own, 'core', [(0, 1), (1, 0)])  6.38 us
    pallas_call x1, Pallas kernels, join(): pl.pallas_call(functools.partial(join_kernel, cap), out_shape=[jax.ShapeD...  6.36 us
    ppermute x2, starting transfers between devices, from_next(): return lax.ppermute(end, PLANE, pairs)  5.43 us
  transfers between devices with their start and end apart: 8, of which 3 were waited for; matrix products, arithmetic and copies ran while one was open for 1% of the time, Pallas kernels for 12%

profile of v2, /device:TPU:6, one launch (start us, length us, event | category | flops | bytes accessed | tf_op | source)
XLA Modules:
  0.0 231.6 jit_solution(5440889617372303417)
XLA Ops:
  6.5 1.8 turn.1
  8.3 0.0 all-gather.2.cloned.1.call-update
  8.3 0.8 reshape.34.bricks_ref
  9.1 3.2 %pack.1 = bf16[1024,1152]{1,0:T(8,128)(2,1)} custom-call(s32[1,512]{1,0:T(1,128)S(1)} %bitcast.13, s32[1,512]{1,0:T(1,128)S(1)} %copy-done.6, bf16[512,1024]{1,0:T(8,128)(2,1)S(1)} %reshape.34.bricks_ref), custom_call_target="tpu_custom_call" | custom-call | flops 1073741824 | bytes 3145728 | tf_op jit(solution)/shard_map/pack/pallas_call | solution.py:60
  12.3 10.2 %all-to-all-start = ((bf16[32,32,1152]{2,1,0:T(8,128)(2,1)}), bf16[32,32,1152]{2,1,0:T(8,128)(2,1)}, u32[]{:S(2)}, u32[]{:S(2)}) async-start(bf16[32,32,1152]{2,1,0:T(8,128)(2,1)} %bitcast.7), calls=%async_computation | async-start | bytes 4718592 | tf_op jit(solution)/shard_map/all_to_all | solution.py:481
  22.7 0.0 reduce-scatter.2.cloned.1.call-start
  22.7 63.9 %all-gather.2.cloned.1.call-done = bf16[256,32,128]{2,1,0:T(8,128)(2,1)} async-done(((bf16[16,32,128]{2,1,0:T(8,128)(2,1)}), bf16[256,32,128]{2,1,0:T(8,128)(2,1)}) %all-gather.2.cloned.1.call-update) | async-done | bytes 2097168 | tf_op jit(solution)/shard_map/all_gather | solution.py:475
  86.7 2.3 dynamic-slice_bitcast_fusion
  88.9 1.9 collective-permute-start.1
  90.9 2.9 %collective-permute-start = (bf16[128,32,128]{2,1,0:T(8,128)(2,1)}, bf16[128,32,128]{2,1,0:T(8,128)(2,1)S(1)}, u32[]{:S(2)}, u32[]{:S(2)}) collective-permute-start(bf16[128,32,128]{2,1,0:T(8,128)(2,1)} %dynamic-slice_bitcast_fusion), channel_id=1, source_target_pairs={{1,4},{5,8},{4,1},{9,12},{8,5},{13,16},{12,9},{17,20},{16,13},{21,... | collective-permute-start | bytes 3145736 | tf_op jit(solution)/shard_map/ppermute | solution.py:446
  93.8 1.1 tables.1
  94.9 6.4 %join.1 = (f32[32,128,128]{2,1,0:T(8,128)S(1)}, f32[32,128,128]{2,1,0:T(8,128)S(1)}) custom-call(s32[1,1]{1,0:T(1,128)} %bitcast.2.core_ref, s32[1,4]{1,0:T(1,128)S(1)} %copy-done.7, f32[1,4]{1,0:T(1,128)S(1)} %copy-done.8, s32[1,2]{1,0:T(1,128)S(1)} %copy-done.9, f32[1,2]{1,0:T(1,128)S(1)} %copy-done.10, s32[1,128]{1,0:T(1,128)S(1)} %copy-done.11, ...), custom_call_target="tpu_custom_call" | custom-call | flops 1342177280 | bytes 6291456 | tf_op jit(solution)/shard_map/join/pallas_call | solution.py:378
  101.3 8.7 %middle.3.inner_ref = bf16[128,32,128]{2,1,0:T(8,128)(2,1)S(1)} custom-call(s32[1]{0:T(128)} %bitcast.1.core_ref, bf16[32,96]{1,0:T(8,128)(2,1)S(1)} %get-tuple-element.16.az_ref, bf16[128,128]{1,0:T(8,128)(2,1)S(1)} %get-tuple-element.17.ay_ref, bf16[256,256]{1,0:T(8,128)(2,1)S(1)} %get-tuple-element.18.ax_ref, ...), custom_call_target="tpu_custom_call" | custom-call | flops 637534208 | bytes 6291456 | tf_op jit(solution)/shard_map/middle/pallas_call | solution.py:268
  110.0 2.6 %collective-permute-start.3 = (bf16[128,32,128]{2,1,0:T(8,128)(2,1)S(1)}, bf16[128,32,128]{2,1,0:T(8,128)(2,1)S(1)}, u32[]{:S(2)}, u32[]{:S(2)}) collective-permute-start(bf16[128,32,128]{2,1,0:T(8,128)(2,1)S(1)} %middle.3.inner_ref), channel_id=1, source_target_pairs={{0,1},{1,0},{2,3},{3,2},{4,5},{5,4},{6,7},{7,6},{8,9},{9,8},{10,11... | collective-permute-start | bytes 3145736 | tf_op jit(solution)/shard_map/ppermute | solution.py:436
  112.5 8.7 %middle.2.outer_ref = bf16[128,32,128]{2,1,0:T(8,128)(2,1)S(1)} custom-call(s32[1]{0:T(128)} %bitcast.1.core_ref, bf16[32,96]{1,0:T(8,128)(2,1)S(1)} %get-tuple-element.16.az_ref, bf16[128,128]{1,0:T(8,128)(2,1)S(1)} %get-tuple-element.17.ay_ref, bf16[256,256]{1,0:T(8,128)(2,1)S(1)} %get-tuple-element.18.ax_ref, ...), custom_call_target="tpu_custom_call" | custom-call | flops 637534208 | bytes 6291456 | tf_op jit(solution)/shard_map/middle/pallas_call | solution.py:268
  121.2 1.9 collective-permute-start.4
  123.2 2.6 %collective-permute-start.2 = (bf16[128,32,128]{2,1,0:T(8,128)(2,1)S(1)}, bf16[128,32,128]{2,1,0:T(8,128)(2,1)S(1)}, u32[]{:S(2)}, u32[]{:S(2)}) collective-permute-start(bf16[128,32,128]{2,1,0:T(8,128)(2,1)S(1)} %middle.2.outer_ref), channel_id=1, source_target_pairs={{1,4},{5,8},{4,1},{9,12},{8,5},{13,16},{12,9},{17,20},{16,13},{21,... | collective-permute-start | bytes 3145736 | tf_op jit(solution)/shard_map/ppermute | solution.py:446
  125.8 0.0 collective-permute-done.4.oth_outer_ref
  125.8 13.5 %collective-permute-done.2.beside_ref = bf16[128,32,128]{2,1,0:T(8,128)(2,1)S(1)} collective-permute-done((bf16[128,32,128]{2,1,0:T(8,128)(2,1)S(1)}, bf16[128,32,128]{2,1,0:T(8,128)(2,1)S(1)}, u32[]{:S(2)}, u32[]{:S(2)}) %collective-permute-start.2) | collective-permute-done | bytes 1048608 | tf_op jit(solution)/shard_map/ppermute | solution.py:446
  139.3 4.4 %back.1 = f32[2,128,32,128]{3,2,1,0:T(8,128)} custom-call(s32[1]{0:T(128)} %bitcast.1.core_ref, bf16[32,96]{1,0:T(8,128)(2,1)S(1)} %get-tuple-element.15.table, bf16[128,32,128]{2,1,0:T(8,128)(2,1)S(1)} %collective-permute-done.2.beside_ref, bf16[128,32,128]{2,1,0:T(8,128)(2,1)S(1)} %middle.2.outer_ref, ...), custom_call_target="tpu_custom_call" | custom-call | flops 201326592 | bytes 9437184 | tf_op jit(solution)/shard_map/back/pallas_call | solution.py:414
  143.7 0.0 reduce-scatter.2.cloned.1.call-update
  143.7 79.3 %reduce-scatter.2.cloned.1.call-done = f32[1,16,32,128]{3,2,1,0:T(8,128)} async-done(((f32[16,16,32,128]{3,2,1,0:T(8,128)}), f32[1,16,32,128]{3,2,1,0:T(8,128)}) %reduce-scatter.2.cloned.1.call-update) | async-done | bytes 262160 | tf_op jit(solution)/shard_map/reduce_scatter | solution.py:501
  223.1 0.9 copy-done.1
  224.0 0.8 finish.1
  (32 shorter events, 0.1 us)
Async XLA Ops:
  6.5 1.8 copy-start.13
  6.5 80.1 %all-gather.2.cloned.1.call-start = ((), (), s32[]{:S(2)}) async-start(), calls=%async_computation.2 | async-start | bytes 2228224 | tf_op jit(solution)/shard_map/all_gather | solution.py:475
  6.5 2.6 %copy-start.5 = (s32[1,512,1]{1,2,0:T(1,128)S(1)}, s32[1,512,1]{1,2,0:T(1,128)}, u32[]{:S(2)}) copy-start(s32[1,512,1]{1,2,0:T(1,128)} %param.15) | copy-start | bytes 6148
  6.5 2.6 %copy-start.6 = (s32[1,512]{1,0:T(1,128)S(1)}, s32[1,512]{1,0:T(1,128)}, u32[]{:S(2)}) copy-start(s32[1,512]{1,0:T(1,128)} %pos_ref.1) | copy-start | bytes 6148
  12.3 82.5 %all-to-all-start = ((bf16[32,32,1152]{2,1,0:T(8,128)(2,1)}), bf16[32,32,1152]{2,1,0:T(8,128)(2,1)}, u32[]{:S(2)}, u32[]{:S(2)}) async-start(bf16[32,32,1152]{2,1,0:T(8,128)(2,1)} %bitcast.7), calls=%async_computation | async-start | bytes 4718592 | tf_op jit(solution)/shard_map/all_to_all | solution.py:481
  22.6 71.2 %copy-start.2 = (f32[1,64]{1,0:T(1,128)S(1)}, f32[1,64]{1,0:T(1,128)}, u32[]{:S(2)}) copy-start(f32[1,64]{1,0:T(1,128)} %psf_z_ref.1) | copy-start | bytes 772
  22.6 71.1 %copy-start.3 = (f32[1,16]{1,0:T(1,128)S(1)}, f32[1,16]{1,0:T(1,128)}, u32[]{:S(2)}) copy-start(f32[1,16]{1,0:T(1,128)} %psf_y_ref.1) | copy-start | bytes 196
  22.6 71.1 %copy-start.4 = (f32[1,16]{1,0:T(1,128)S(1)}, f32[1,16]{1,0:T(1,128)}, u32[]{:S(2)}) copy-start(f32[1,16]{1,0:T(1,128)} %psf_x_ref.1) | copy-start | bytes 196
  22.6 72.2 %copy-start.7 = (s32[1,4]{1,0:T(1,128)S(1)}, s32[1,4]{1,0:T(1,128)}, u32[]{:S(2)}) copy-start(s32[1,4]{1,0:T(1,128)} %off_z_ref.1) | copy-start | bytes 52
  22.6 72.2 %copy-start.8 = (f32[1,4]{1,0:T(1,128)S(1)}, f32[1,4]{1,0:T(1,128)}, u32[]{:S(2)}) copy-start(f32[1,4]{1,0:T(1,128)} %frac_z_ref.1) | copy-start | bytes 52
  22.6 72.2 %copy-start.9 = (s32[1,2]{1,0:T(1,128)S(1)}, s32[1,2]{1,0:T(1,128)}, u32[]{:S(2)}) copy-start(s32[1,2]{1,0:T(1,128)} %off_y_ref.1) | copy-start | bytes 28
  22.6 72.2 %copy-start.10 = (f32[1,2]{1,0:T(1,128)S(1)}, f32[1,2]{1,0:T(1,128)}, u32[]{:S(2)}) copy-start(f32[1,2]{1,0:T(1,128)} %frac_y_ref.1) | copy-start | bytes 28
  22.7 72.2 %copy-start.11 = (s32[1,128]{1,0:T(1,128)S(1)}, s32[1,128]{1,0:T(1,128)}, u32[]{:S(2)}) copy-start(s32[1,128]{1,0:T(1,128)} %off_x_ref.1) | copy-start | bytes 1540
  22.7 72.2 %copy-start.12 = (f32[1,128]{1,0:T(1,128)S(1)}, f32[1,128]{1,0:T(1,128)}, u32[]{:S(2)}) copy-start(f32[1,128]{1,0:T(1,128)} %frac_x_ref.1) | copy-start | bytes 1540
  22.7 200.4 %reduce-scatter.2.cloned.1.call-start = ((), (), s32[]{:S(2)}) async-start(), calls=%async_computation.3 | async-start | bytes 4456448 | tf_op jit(solution)/shard_map/reduce_scatter | solution.py:501
  88.9 12.3 %collective-permute-start.1 = (bf16[2,128,32,128]{3,2,1,0:T(8,128)(2,1)}, bf16[2,128,32,128]{3,2,1,0:T(8,128)(2,1)S(1)}, u32[]{:S(2)}, u32[]{:S(2)}) collective-permute-start(bf16[2,128,32,128]{3,2,1,0:T(8,128)(2,1)} %bitcast.3.own_ref), channel_id=1, source_target_pairs={{0,1},{1,0},{2,3},{3,2},{4,5},{5,4},{6,7},{7,6},{8,9},{9,8},{10,11... | collective-permute-start | bytes 6291464 | tf_op jit(solution)/shard_map/ppermute | solution.py:436
  90.9 21.7 %collective-permute-start = (bf16[128,32,128]{2,1,0:T(8,128)(2,1)}, bf16[128,32,128]{2,1,0:T(8,128)(2,1)S(1)}, u32[]{:S(2)}, u32[]{:S(2)}) collective-permute-start(bf16[128,32,128]{2,1,0:T(8,128)(2,1)} %dynamic-slice_bitcast_fusion), channel_id=1, source_target_pairs={{1,4},{5,8},{4,1},{9,12},{8,5},{13,16},{12,9},{17,20},{16,13},{21,... | collective-permute-start | bytes 3145736 | tf_op jit(solution)/shard_map/ppermute | solution.py:446
  110.0 15.8 %collective-permute-start.3 = (bf16[128,32,128]{2,1,0:T(8,128)(2,1)S(1)}, bf16[128,32,128]{2,1,0:T(8,128)(2,1)S(1)}, u32[]{:S(2)}, u32[]{:S(2)}) collective-permute-start(bf16[128,32,128]{2,1,0:T(8,128)(2,1)S(1)} %middle.3.inner_ref), channel_id=1, source_target_pairs={{0,1},{1,0},{2,3},{3,2},{4,5},{5,4},{6,7},{7,6},{8,9},{9,8},{10,11... | collective-permute-start | bytes 3145736 | tf_op jit(solution)/shard_map/ppermute | solution.py:436
  121.2 4.6 %collective-permute-start.4 = (bf16[128,32,128]{2,1,0:T(8,128)(2,1)S(1)}, bf16[128,32,128]{2,1,0:T(8,128)(2,1)S(1)}, u32[]{:S(2)}, u32[]{:S(2)}) collective-permute-start(bf16[128,32,128]{2,1,0:T(8,128)(2,1)S(1)} %middle.2.outer_ref), channel_id=1, source_target_pairs={{0,1},{1,0},{2,3},{3,2},{4,5},{5,4},{6,7},{7,6},{8,9},{9,8},{10,11... | collective-permute-start | bytes 3145736 | tf_op jit(solution)/shard_map/ppermute | solution.py:436
  123.2 16.1 %collective-permute-start.2 = (bf16[128,32,128]{2,1,0:T(8,128)(2,1)S(1)}, bf16[128,32,128]{2,1,0:T(8,128)(2,1)S(1)}, u32[]{:S(2)}, u32[]{:S(2)}) collective-permute-start(bf16[128,32,128]{2,1,0:T(8,128)(2,1)S(1)} %middle.2.outer_ref), channel_id=1, source_target_pairs={{1,4},{5,8},{4,1},{9,12},{8,5},{13,16},{12,9},{17,20},{16,13},{21,... | collective-permute-start | bytes 3145736 | tf_op jit(solution)/shard_map/ppermute | solution.py:446
  143.7 79.3 %copy-start = (f32[32,128,128]{2,1,0:T(8,128)S(1)}, f32[32,128,128]{2,1,0:T(8,128)}, u32[]{:S(2)}) copy-start(f32[32,128,128]{2,1,0:T(8,128)} %part_ref.3) | copy-start | bytes 6291460
  223.1 1.0 copy-start.1
Sparse Core Ops, SparseCore 0:
  9.4 77.1 all-gather.1
  143.9 79.1 reduce-scatter.1

commit v3 on v2

--- a/solution.py
+++ b/solution.py
@@ -139,7 +139,6 @@
             ],
             out_specs=pl.BlockSpec((depth, share, cols), lambda i, view: (0, 0, 0)),
         ),
-        compiler_params=pltpu.CompilerParams(vmem_limit_bytes=8 * MIB),
         cost_estimate=pl.CostEstimate(
             flops=0, bytes_accessed=12 * depth * share * cols, transcendentals=0
         ),
@@ -181,7 +180,24 @@
     )(core, psf_z, psf_y, psf_x)
 
 
+def pick_kernel(core_ref, own_ref, out_ref):
+    pltpu.sync_copy(own_ref.at[core_ref[0]], out_ref)
+
+
+def pick(core, own):
+    return pl.pallas_call(
+        pick_kernel,
+        out_shape=jax.ShapeDtypeStruct(own.shape[1:], own.dtype),
+        in_specs=[pl.BlockSpec(memory_space=SMEM), pl.BlockSpec(memory_space=pltpu.HBM)],
+        out_specs=pl.BlockSpec(memory_space=VMEM),
+        compiler_params=pltpu.CompilerParams(vmem_limit_bytes=4 * MIB),
+        cost_estimate=pl.CostEstimate(flops=0, bytes_accessed=2 * own.size, transcendentals=0),
+        name="pick",
+    )(core, own)
+
+
 def middle_kernel(
+    picks,
     core_ref,
     az_ref,
     ay_ref,
@@ -199,6 +215,9 @@
     res,
 ):
     rows, depth, cols = out_ref.shape
+    one_ref, two_ref = (
+        ref.at[which(core_ref[0])] for ref, which in zip((one_ref, two_ref), picks, strict=True)
+    )
 
     def column(y):
         return jnp.concatenate([one_ref[y], own_ref[y], two_ref[y]], axis=0)
@@ -262,22 +281,18 @@
 
 def middle(core, weights, one, own, two, joined):
     _, rows, depth, cols = own[0].shape
-    slab = (None, rows, depth, cols)
     points = depth * rows * cols
     half = (depth * rows // 2, 2 * cols)
-    return pl.pallas_call(
-        middle_kernel,
+    whole = pl.BlockSpec(memory_space=VMEM)
+    own_spec = pl.BlockSpec((None, rows, depth, cols), lambda i, core: (own[1](core[0]), 0, 0, 0))
+    return pl.pallas_call(
+        functools.partial(middle_kernel, (one[1], two[1])),
         out_shape=jax.ShapeDtypeStruct((rows, depth, cols), BF),
         grid_spec=pltpu.PrefetchScalarGridSpec(
             num_scalar_prefetch=1,
             grid=(1,),
-            in_specs=[pl.BlockSpec(w.shape, lambda i, core: (0, 0)) for w in weights]
-            + [
-                pl.BlockSpec(slab, lambda i, core, which=which: (which(core[0]), 0, 0, 0))
-                for _, which in (one, own, two)
-            ]
-            + [pl.BlockSpec((depth, rows, cols), lambda i, core: (0, 0, 0))],
-            out_specs=pl.BlockSpec((rows, depth, cols), lambda i, core: (0, 0, 0)),
+            in_specs=[whole] * (len(weights) + 1) + [own_spec] + [whole] * 2,
+            out_specs=whole,
             scratch_shapes=[
                 pltpu.VMEM((depth, rows, cols), F32),
                 pltpu.VMEM(half, BF),
@@ -285,7 +300,7 @@
                 pltpu.VMEM((rows, depth, cols), F32),
             ],
         ),
-        compiler_params=pltpu.CompilerParams(vmem_limit_bytes=28 * MIB),
+        compiler_params=pltpu.CompilerParams(vmem_limit_bytes=20 * MIB),
         cost_estimate=pl.CostEstimate(
             flops=2 * points * (3 * depth + 2 * rows + 2 * cols),
             bytes_accessed=12 * points,
@@ -381,7 +396,7 @@
         in_specs=[pl.BlockSpec(memory_space=SMEM)] * 5 + [pl.BlockSpec(memory_space=VMEM)] * 3,
         out_specs=[pl.BlockSpec(memory_space=VMEM)] * 2,
         scratch_shapes=[pltpu.VMEM((points, cols), BF)],
-        compiler_params=pltpu.CompilerParams(vmem_limit_bytes=28 * MIB),
+        compiler_params=pltpu.CompilerParams(vmem_limit_bytes=20 * MIB),
         cost_estimate=pl.CostEstimate(
             flops=2 * 2 * points * (slots + cols) * cols,
             bytes_accessed=12 * points * cols,
@@ -429,7 +444,9 @@
 
 
 PLANE = ("y", "x", "core")
-RING = ("zh", "view")
+VIEW = ("vh", "vl")
+COARSE = ("zh", "vh")
+RING = ("zh", "vh", "vl")
 
 
 def swapped(own):
@@ -465,37 +482,37 @@
 ):
     depth, rows, cols = estimate.shape
     count = raw_bricks.shape[1]
-    views = lax.axis_size("view")
+    views = lax.axis_size(VIEW)
     share = rows // views
     core = lax.axis_index("core").astype(I32)
-    view = lax.axis_index("view").astype(I32)
+    view = lax.axis_index(VIEW).astype(I32)
     place = core.reshape(1)
 
-    piece = turn(view.reshape(1), estimate, share)
-    own = lax.all_gather(piece, RING, axis=0, tiled=True).reshape(2, rows, depth, cols)
+    piece = turn(lax.axis_index("vh").astype(I32).reshape(1), estimate, rows // lax.axis_size("vh"))
+    own = lax.all_gather(piece, COARSE, axis=0, tiled=True).reshape(2, rows, depth, cols)
 
     packed = pack(
         brick_slab.reshape(1, count), brick_pos, raw_bricks.reshape(count, -1), cap, chips
     )
     packed = packed.reshape(2 * chips, 2 * cap, -1)
     arrived = lax.all_to_all(packed, PLANE, split_axis=0, concat_axis=0, tiled=True)
-    joined_inner, joined_outer = join(
+    weights = tables(core.reshape(1, 1), psf_z, psf_y, psf_x, depth, rows, cols)
+    joined = join(
         cap, rows, depth, core.reshape(1, 1), off_z, frac_z, off_y, frac_y, off_x, frac_x, arrived
     )
-
-    end = lax.dynamic_index_in_dim(own, core, 0, keepdims=False)
-    own, end = lax.optimization_barrier((own, end))
-    beside = from_next(end, chips)[None]
+    own, weights, joined = lax.optimization_barrier((own, weights, joined))
+    az, ay, ax, bz, by, bx = weights
+    weights = (az, ay, ax, by, bx)
+    joined_inner, joined_outer = joined
+
+    same, flip, first = (lambda c: c), (lambda c: 1 - c), (lambda c: 0)
     oth = swapped(own)
-    az, ay, ax, bz, by, bx = tables(core.reshape(1, 1), psf_z, psf_y, psf_x, depth, rows, cols)
-    weights = (az, ay, ax, by, bx)
-    same, flip, first = (lambda c: c), (lambda c: 1 - c), (lambda c: 0)
+    beside = from_next(pick(place, own), chips)[None]
     inner = middle(place, weights, (oth, same), (own, flip), (oth, flip), joined_inner)
     outer = middle(place, weights, (beside, first), (own, same), (oth, same), joined_outer)
-
-    oth_inner = swapped(inner)
     beside = from_next(outer, chips)
     oth_outer = swapped(outer)
+    oth_inner = swapped(inner)
     correction = back(place, bz, beside, outer, oth_inner, inner, oth_outer, share)
     correction = correction.reshape(2 * views, share, depth, cols)
     total = lax.psum_scatter(correction, RING, scatter_dimension=0, tiled=True)
@@ -505,15 +522,16 @@
 def solution(mesh):
     devices = mesh.devices
     views, slabs = devices.shape
-    fine = Mesh(devices.reshape(views, 4, slabs // 16, 2, 2), ("view", "y", "x", "zh", "core"))
+    names = ("vh", "vl", "y", "x", "zh", "core")
+    fine = Mesh(devices.reshape(views // 2, 2, 4, slabs // 16, 2, 2), names)
     gz = ("y", "x", "zh", "core")
     in_specs = (
         P(gz, None, None),
-        P("view", gz, None, None, None),
-        P("view", gz, None),
-        P("view", gz),
-    ) + (P("view", None),) * 9
-    out_specs = P(gz, "view", None)
+        P(VIEW, gz, None, None, None),
+        P(VIEW, gz, None),
+        P(VIEW, gz),
+    ) + (P(VIEW, None),) * 9
+    out_specs = P(gz, VIEW, None)
     return jax.shard_map(
         functools.partial(shards, slabs // 4, 16),
         mesh=fine,

time: 232 us -> 219 us (0.944)
  waiting for transfers between devices: 157 us -> 141 us
  local copies, waits for them, and re-layouts: 4.07 us -> 8.09 us
  Pallas kernels: 35 us -> 31.3 us
    all_gather x1, waiting for transfers between devices: 63.9 us -> 20.5 us  [shards(): lax.all_gather(piece, COARSE, axis=0, tiled=True)]
    all_to_all x1, waiting for transfers between devices: 0.01 us -> 27.5 us  [shards(): lax.all_to_all(packed, PLANE, split_axis=0, concat_axis=0, tiled=True)]
    unnamed x28 -> x38, local copies, waits for them, and re-layouts: 1.02 us -> 7.33 us
    ppermute x3, starting transfers between devices: 6.38 us -> 9.41 us  [swapped(): return lax.ppermute(own, 'core', [(0, 1), (1, 0)])]
    pallas_call x2 -> x3, Pallas kernels: 17.4 us -> 15 us  [the longest x2 14.9 us: middle(): pl.pallas_call(functools.partial(middle_kernel, (one[1], two[1])), out_sh...]
  transfers between devices with their start and end apart: 8 -> 8, of which waited for: 3 -> 6; matrix products, arithmetic and copies ran while one was open for 1% -> 0% of each run, Pallas kernels for 12% -> 11%
where the time goes in v3:
time: 219 us; the launch traced here: 218 us
  waiting for transfers between devices  141 us (64%)
  Pallas kernels  31.3 us (14%)
  starting transfers between devices  24.4 us (11%)
  between operations  13.7 us (6%)
  local copies, waits for them, and re-layouts  8.09 us (4%)
    reduce_scatter x1, waiting for transfers between devices, shards(): total = lax.psum_scatter(correction, RING, scatter_dimension=0, tiled=True)  77.6 us
    all_to_all x1, waiting for transfers between devices, shards(): lax.all_to_all(packed, PLANE, split_axis=0, concat_axis=0, tiled=True)  27.5 us
    all_gather x1, waiting for transfers between devices, shards(): lax.all_gather(piece, COARSE, axis=0, tiled=True)  20.5 us
    pallas_call x2, Pallas kernels, middle(): pl.pallas_call(functools.partial(middle_kernel, (one[1], two[1])), out_sh...  14.9 us
    ppermute x2, waiting for transfers between devices, from_next(): return lax.ppermute(end, PLANE, pairs)  14.8 us
    all_to_all x1, starting transfers between devices, shards(): lax.all_to_all(packed, PLANE, split_axis=0, concat_axis=0, tiled=True)  9.71 us
    ppermute x3, starting transfers between devices, swapped(): return lax.ppermute(own, 'core', [(0, 1), (1, 0)])  9.41 us
    unnamed x38, local copies, waits for them, and re-layouts  7.33 us
  transfers between devices with their start and end apart: 8, of which 6 were waited for; matrix products, arithmetic and copies ran while one was open for 0% of the time, Pallas kernels for 11%

profile of v3, /device:TPU:6, one launch (start us, length us, event | category | flops | bytes accessed | tf_op | source)
XLA Modules:
  0.0 218.2 jit_solution(2218828892628207719)
XLA Ops:
  6.5 2.0 turn.1
  9.3 1.7 pack.1
  11.1 1.4 copy-done.2
  12.6 9.7 %all-to-all-start = ((bf16[32,32,1152]{2,1,0:T(8,128)(2,1)}), bf16[32,32,1152]{2,1,0:T(8,128)(2,1)S(1)}, u32[]{:S(2)}, u32[]{:S(2)}) async-start(bf16[32,32,1152]{2,1,0:T(8,128)(2,1)} %bitcast.14), calls=%async_computation | async-start | bytes 4718592 | tf_op jit(solution)/shard_map/all_to_all | solution.py:498
  22.4 1.1 tables.1
  23.4 27.5 %all-to-all-done.arrived_ref = bf16[32,32,1152]{2,1,0:T(8,128)(2,1)S(1)} async-done(((bf16[32,32,1152]{2,1,0:T(8,128)(2,1)}), bf16[32,32,1152]{2,1,0:T(8,128)(2,1)S(1)}, u32[]{:S(2)}, u32[]{:S(2)}) %all-to-all-start) | async-done | bytes 2359328 | tf_op jit(solution)/shard_map/all_to_all | solution.py:498
  50.9 5.2 %join.1 = (f32[32,128,128]{2,1,0:T(8,128)S(1)}, f32[32,128,128]{2,1,0:T(8,128)S(1)}) custom-call(s32[1,1]{1,0:T(1,128)} %bitcast.4.core_ref, s32[1,4]{1,0:T(1,128)S(1)} %copy-done.12, f32[1,4]{1,0:T(1,128)S(1)} %copy-done.13, s32[1,2]{1,0:T(1,128)S(1)} %copy-done.14, f32[1,2]{1,0:T(1,128)S(1)} %copy-done.15, s32[1,128]{1,0:T(1,128)S(1)} %copy-done.16, ...), custom_call_target="tpu_custom_call" | custom-call | flops 1342177280 | bytes 6291456 | tf_op jit(solution)/shard_map/join/pallas_call | solution.py:393
  56.2 1.3 copy-done.3
  57.5 1.4 copy-done.5
  58.9 20.5 %all-gather.2.cloned.1.call-done = bf16[256,32,128]{2,1,0:T(8,128)(2,1)} async-done(((bf16[32,32,128]{2,1,0:T(8,128)(2,1)}), bf16[256,32,128]{2,1,0:T(8,128)(2,1)}) %all-gather.2.cloned.1.call-update) | async-done | bytes 2097168 | tf_op jit(solution)/shard_map/all_gather | solution.py:492
  79.4 1.9 collective-permute-start.1
  81.3 1.6 copy-done
  83.0 3.4 %collective-permute-start = (bf16[128,32,128]{2,1,0:T(8,128)(2,1)S(1)}, bf16[128,32,128]{2,1,0:T(8,128)(2,1)S(1)}, u32[]{:S(2)}, u32[]{:S(2)}) collective-permute-start(bf16[128,32,128]{2,1,0:T(8,128)(2,1)S(1)} %pick.1), channel_id=1, source_target_pairs={{1,4},{5,8},{4,1},{9,12},{8,5},{13,16},{12,9},{17,20},{16,13},{21,... | collective-permute-start | bytes 3145736 | tf_op jit(solution)/shard_map/ppermute | solution.py:463
  86.4 1.6 copy-done.6
  87.9 7.5 %middle.3.inner_ref = bf16[128,32,128]{2,1,0:T(8,128)(2,1)S(1)} custom-call(s32[1]{0:T(128)} %bitcast.1.core_ref, bf16[32,96]{1,0:T(8,128)(2,1)S(1)} %get-tuple-element.31.az_ref, bf16[128,128]{1,0:T(8,128)(2,1)S(1)} %get-tuple-element.32.ay_ref, bf16[256,256]{1,0:T(8,128)(2,1)S(1)} %get-tuple-element.33.ax_ref, ...), custom_call_target="tpu_custom_call" | custom-call | flops 637534208 | bytes 6291456 | tf_op jit(solution)/shard_map/middle/pallas_call | solution.py:288
  95.4 3.0 %collective-permute-start.3 = (bf16[128,32,128]{2,1,0:T(8,128)(2,1)S(1)}, bf16[128,32,128]{2,1,0:T(8,128)(2,1)S(1)}, u32[]{:S(2)}, u32[]{:S(2)}) collective-permute-start(bf16[128,32,128]{2,1,0:T(8,128)(2,1)S(1)} %middle.3.inner_ref), channel_id=1, source_target_pairs={{0,1},{1,0},{2,3},{3,2},{4,5},{5,4},{6,7},{7,6},{8,9},{9,8},{10,11... | collective-permute-start | bytes 3145736 | tf_op jit(solution)/shard_map/ppermute | solution.py:453
  98.4 0.9 collective-permute-done
  99.3 7.5 %middle.2.outer_ref = bf16[128,32,128]{2,1,0:T(8,128)(2,1)S(1)} custom-call(s32[1]{0:T(128)} %bitcast.1.core_ref, bf16[32,96]{1,0:T(8,128)(2,1)S(1)} %get-tuple-element.31.az_ref, bf16[128,128]{1,0:T(8,128)(2,1)S(1)} %get-tuple-element.32.ay_ref, bf16[256,256]{1,0:T(8,128)(2,1)S(1)} %get-tuple-element.33.ax_ref, ...), custom_call_target="tpu_custom_call" | custom-call | flops 637534208 | bytes 6291456 | tf_op jit(solution)/shard_map/middle/pallas_call | solution.py:288
  106.8 4.5 %collective-permute-start.4 = (bf16[128,32,128]{2,1,0:T(8,128)(2,1)S(1)}, bf16[128,32,128]{2,1,0:T(8,128)(2,1)S(1)}, u32[]{:S(2)}, u32[]{:S(2)}) collective-permute-start(bf16[128,32,128]{2,1,0:T(8,128)(2,1)S(1)} %middle.2.outer_ref), channel_id=1, source_target_pairs={{0,1},{1,0},{2,3},{3,2},{4,5},{5,4},{6,7},{7,6},{8,9},{9,8},{10,11... | collective-permute-start | bytes 3145736 | tf_op jit(solution)/shard_map/ppermute | solution.py:453
  111.4 1.9 collective-permute-start.2
  113.6 13.9 %collective-permute-done.2.beside_ref = bf16[128,32,128]{2,1,0:T(8,128)(2,1)S(1)} collective-permute-done((bf16[128,32,128]{2,1,0:T(8,128)(2,1)S(1)}, bf16[128,32,128]{2,1,0:T(8,128)(2,1)S(1)}, u32[]{:S(2)}, u32[]{:S(2)}) %collective-permute-start.2) | collective-permute-done | bytes 1048608 | tf_op jit(solution)/shard_map/ppermute | solution.py:463
  127.5 4.5 %back.1 = f32[2,128,32,128]{3,2,1,0:T(8,128)} custom-call(s32[1]{0:T(128)} %bitcast.1.core_ref, bf16[32,96]{1,0:T(8,128)(2,1)S(1)} %get-tuple-element.30.table, bf16[128,32,128]{2,1,0:T(8,128)(2,1)S(1)} %collective-permute-done.2.beside_ref, bf16[128,32,128]{2,1,0:T(8,128)(2,1)S(1)} %middle.2.outer_ref, ...), custom_call_target="tpu_custom_call" | custom-call | flops 201326592 | bytes 9437184 | tf_op jit(solution)/shard_map/back/pallas_call | solution.py:429
  132.0 77.6 %reduce-scatter.2.cloned.1.call-done = f32[1,16,32,128]{3,2,1,0:T(8,128)} async-done(((f32[16,16,32,128]{3,2,1,0:T(8,128)}), f32[1,16,32,128]{3,2,1,0:T(8,128)}) %reduce-scatter.2.cloned.1.call-update) | async-done | bytes 262160 | tf_op jit(solution)/shard_map/reduce_scatter | solution.py:518
  209.6 1.8 finish.1
  (42 shorter events, 1.3 us)
Async XLA Ops:
  6.5 2.0 copy-start.18
  6.5 72.8 %all-gather.2.cloned.1.call-start = ((), (), s32[]{:S(2)}) async-start(), calls=%async_computation.2 | async-start | bytes 2359296 | tf_op jit(solution)/shard_map/all_gather | solution.py:492
  6.5 2.8 %copy-start.10 = (s32[1,512,1]{1,2,0:T(1,128)S(1)}, s32[1,512,1]{1,2,0:T(1,128)}, u32[]{:S(2)}) copy-start(s32[1,512,1]{1,2,0:T(1,128)} %param.15) | copy-start | bytes 6148
  6.5 2.8 %copy-start.11 = (s32[1,512]{1,0:T(1,128)S(1)}, s32[1,512]{1,0:T(1,128)}, u32[]{:S(2)}) copy-start(s32[1,512]{1,0:T(1,128)} %pos_ref.1) | copy-start | bytes 6148
  12.5 9.8 %copy-start.7 = (f32[1,64]{1,0:T(1,128)S(1)}, f32[1,64]{1,0:T(1,128)}, u32[]{:S(2)}) copy-start(f32[1,64]{1,0:T(1,128)} %psf_z_ref.1) | copy-start | bytes 772
  12.5 9.9 %copy-start.8 = (f32[1,16]{1,0:T(1,128)S(1)}, f32[1,16]{1,0:T(1,128)}, u32[]{:S(2)}) copy-start(f32[1,16]{1,0:T(1,128)} %psf_y_ref.1) | copy-start | bytes 196
  12.5 9.9 %copy-start.9 = (f32[1,16]{1,0:T(1,128)S(1)}, f32[1,16]{1,0:T(1,128)}, u32[]{:S(2)}) copy-start(f32[1,16]{1,0:T(1,128)} %psf_x_ref.1) | copy-start | bytes 196
  12.5 38.4 %copy-start.12 = (s32[1,4]{1,0:T(1,128)S(1)}, s32[1,4]{1,0:T(1,128)}, u32[]{:S(2)}) copy-start(s32[1,4]{1,0:T(1,128)} %off_z_ref.1) | copy-start | bytes 52
  12.5 38.4 %copy-start.13 = (f32[1,4]{1,0:T(1,128)S(1)}, f32[1,4]{1,0:T(1,128)}, u32[]{:S(2)}) copy-start(f32[1,4]{1,0:T(1,128)} %frac_z_ref.1) | copy-start | bytes 52
  12.5 38.4 %copy-start.14 = (s32[1,2]{1,0:T(1,128)S(1)}, s32[1,2]{1,0:T(1,128)}, u32[]{:S(2)}) copy-start(s32[1,2]{1,0:T(1,128)} %off_y_ref.1) | copy-start | bytes 28
  12.5 38.4 %copy-start.15 = (f32[1,2]{1,0:T(1,128)S(1)}, f32[1,2]{1,0:T(1,128)}, u32[]{:S(2)}) copy-start(f32[1,2]{1,0:T(1,128)} %frac_y_ref.1) | copy-start | bytes 28
  12.5 38.4 %copy-start.16 = (s32[1,128]{1,0:T(1,128)S(1)}, s32[1,128]{1,0:T(1,128)}, u32[]{:S(2)}) copy-start(s32[1,128]{1,0:T(1,128)} %off_x_ref.1) | copy-start | bytes 1540
  12.5 38.4 %copy-start.17 = (f32[1,128]{1,0:T(1,128)S(1)}, f32[1,128]{1,0:T(1,128)}, u32[]{:S(2)}) copy-start(f32[1,128]{1,0:T(1,128)} %frac_x_ref.1) | copy-start | bytes 1540
  12.6 38.3 %all-to-all-start = ((bf16[32,32,1152]{2,1,0:T(8,128)(2,1)}), bf16[32,32,1152]{2,1,0:T(8,128)(2,1)S(1)}, u32[]{:S(2)}, u32[]{:S(2)}) async-start(bf16[32,32,1152]{2,1,0:T(8,128)(2,1)} %bitcast.14), calls=%async_computation | async-start | bytes 4718592 | tf_op jit(solution)/shard_map/all_to_all | solution.py:498
  22.3 187.3 %reduce-scatter.2.cloned.1.call-start = ((), (), s32[]{:S(2)}) async-start(), calls=%async_computation.3 | async-start | bytes 4456448 | tf_op jit(solution)/shard_map/reduce_scatter | solution.py:518
  79.4 7.0 %collective-permute-start.1 = (bf16[2,128,32,128]{3,2,1,0:T(8,128)(2,1)}, bf16[2,128,32,128]{3,2,1,0:T(8,128)(2,1)S(1)}, u32[]{:S(2)}, u32[]{:S(2)}) collective-permute-start(bf16[2,128,32,128]{3,2,1,0:T(8,128)(2,1)} %bitcast.10), channel_id=1, source_target_pairs={{0,1},{1,0},{2,3},{3,2},{4,5},{5,4},{6,7},{7,6},{8,9},{9,8},{10,11... | collective-permute-start | bytes 6291464 | tf_op jit(solution)/shard_map/ppermute | solution.py:453
  81.3 1.6 copy-start
  82.9 3.5 %copy-start.1 = (bf16[256,32,128]{2,1,0:T(8,128)(2,1)S(1)}, bf16[256,32,128]{2,1,0:T(8,128)(2,1)}, u32[]{:S(2)}) copy-start(bf16[256,32,128]{2,1,0:T(8,128)(2,1)} %all-gather.2.cloned.1.call-done) | copy-start | bytes 6291460
  83.0 16.4 %copy-start.4 = (f32[32,128,128]{2,1,0:T(8,128)S(1)}, f32[32,128,128]{2,1,0:T(8,128)}, u32[]{:S(2)}) copy-start(f32[32,128,128]{2,1,0:T(8,128)} %copy-done.3) | copy-start | bytes 6291460
  83.0 16.4 %collective-permute-start = (bf16[128,32,128]{2,1,0:T(8,128)(2,1)S(1)}, bf16[128,32,128]{2,1,0:T(8,128)(2,1)S(1)}, u32[]{:S(2)}, u32[]{:S(2)}) collective-permute-start(bf16[128,32,128]{2,1,0:T(8,128)(2,1)S(1)} %pick.1), channel_id=1, source_target_pairs={{1,4},{5,8},{4,1},{9,12},{8,5},{13,16},{12,9},{17,20},{16,13},{21,... | collective-permute-start | bytes 3145736 | tf_op jit(solution)/shard_map/ppermute | solution.py:463
  86.4 1.6 copy-start.6
  95.4 17.9 %collective-permute-start.3 = (bf16[128,32,128]{2,1,0:T(8,128)(2,1)S(1)}, bf16[128,32,128]{2,1,0:T(8,128)(2,1)S(1)}, u32[]{:S(2)}, u32[]{:S(2)}) collective-permute-start(bf16[128,32,128]{2,1,0:T(8,128)(2,1)S(1)} %middle.3.inner_ref), channel_id=1, source_target_pairs={{0,1},{1,0},{2,3},{3,2},{4,5},{5,4},{6,7},{7,6},{8,9},{9,8},{10,11... | collective-permute-start | bytes 3145736 | tf_op jit(solution)/shard_map/ppermute | solution.py:453
  106.8 6.8 %collective-permute-start.4 = (bf16[128,32,128]{2,1,0:T(8,128)(2,1)S(1)}, bf16[128,32,128]{2,1,0:T(8,128)(2,1)S(1)}, u32[]{:S(2)}, u32[]{:S(2)}) collective-permute-start(bf16[128,32,128]{2,1,0:T(8,128)(2,1)S(1)} %middle.2.outer_ref), channel_id=1, source_target_pairs={{0,1},{1,0},{2,3},{3,2},{4,5},{5,4},{6,7},{7,6},{8,9},{9,8},{10,11... | collective-permute-start | bytes 3145736 | tf_op jit(solution)/shard_map/ppermute | solution.py:453
  111.4 16.1 %collective-permute-start.2 = (bf16[128,32,128]{2,1,0:T(8,128)(2,1)S(1)}, bf16[128,32,128]{2,1,0:T(8,128)(2,1)S(1)}, u32[]{:S(2)}, u32[]{:S(2)}) collective-permute-start(bf16[128,32,128]{2,1,0:T(8,128)(2,1)S(1)} %middle.2.outer_ref), channel_id=1, source_target_pairs={{1,4},{5,8},{4,1},{9,12},{8,5},{13,16},{12,9},{17,20},{16,13},{21,... | collective-permute-start | bytes 3145736 | tf_op jit(solution)/shard_map/ppermute | solution.py:463
  (3 other events, 4.1 us)
Sparse Core Ops, SparseCore 0:
  9.4 69.9 all-gather.1
  132.1 77.4 reduce-scatter.1

commit v4 on v3

--- a/solution.py
+++ b/solution.py
@@ -215,8 +215,9 @@
     res,
 ):
     rows, depth, cols = out_ref.shape
-    one_ref, two_ref = (
-        ref.at[which(core_ref[0])] for ref, which in zip((one_ref, two_ref), picks, strict=True)
+    one_ref, own_ref, two_ref = (
+        ref.at[which(core_ref[0])]
+        for ref, which in zip((one_ref, own_ref, two_ref), picks, strict=True)
     )
 
     def column(y):
@@ -284,14 +285,13 @@
     points = depth * rows * cols
     half = (depth * rows // 2, 2 * cols)
     whole = pl.BlockSpec(memory_space=VMEM)
-    own_spec = pl.BlockSpec((None, rows, depth, cols), lambda i, core: (own[1](core[0]), 0, 0, 0))
-    return pl.pallas_call(
-        functools.partial(middle_kernel, (one[1], two[1])),
+    return pl.pallas_call(
+        functools.partial(middle_kernel, (one[1], own[1], two[1])),
         out_shape=jax.ShapeDtypeStruct((rows, depth, cols), BF),
         grid_spec=pltpu.PrefetchScalarGridSpec(
             num_scalar_prefetch=1,
             grid=(1,),
-            in_specs=[whole] * (len(weights) + 1) + [own_spec] + [whole] * 2,
+            in_specs=[whole] * (len(weights) + 4),
             out_specs=whole,
             scratch_shapes=[
                 pltpu.VMEM((depth, rows, cols), F32),

time: 219 us -> 219 us (level)
  no operation moved by 1% of the time
where the time goes in v4:
time: 219 us; the launch traced here: 218 us
  waiting for transfers between devices  141 us (64%)
  Pallas kernels  31.3 us (14%)
  starting transfers between devices  24.4 us (11%)
  between operations  13.7 us (6%)
  local copies, waits for them, and re-layouts  8.09 us (4%)
    reduce_scatter x1, waiting for transfers between devices, shards(): total = lax.psum_scatter(correction, RING, scatter_dimension=0, tiled=True)  77.6 us
    all_to_all x1, waiting for transfers between devices, shards(): lax.all_to_all(packed, PLANE, split_axis=0, concat_axis=0, tiled=True)  27.5 us
    all_gather x1, waiting for transfers between devices, shards(): lax.all_gather(piece, COARSE, axis=0, tiled=True)  20.5 us
    pallas_call x2, Pallas kernels, middle(): pl.pallas_call(functools.partial(middle_kernel, (one[1], own[1], two[1]))...  14.9 us
    ppermute x2, waiting for transfers between devices, from_next(): return lax.ppermute(end, PLANE, pairs)  14.8 us
    all_to_all x1, starting transfers between devices, shards(): lax.all_to_all(packed, PLANE, split_axis=0, concat_axis=0, tiled=True)  9.71 us
    ppermute x3, starting transfers between devices, swapped(): return lax.ppermute(own, 'core', [(0, 1), (1, 0)])  9.41 us
    unnamed x38, local copies, waits for them, and re-layouts  7.33 us
  transfers between devices with their start and end apart: 8, of which 6 were waited for; matrix products, arithmetic and copies ran while one was open for 0% of the time, Pallas kernels for 11%

profile of v4, /device:TPU:6, one launch (start us, length us, event | category | flops | bytes accessed | tf_op | source)
XLA Modules:
  0.0 218.2 jit_solution(1404799464457330216)
XLA Ops:
  6.5 2.0 turn.1
  9.3 1.7 pack.1
  11.1 1.4 copy-done.2
  12.6 9.7 %all-to-all-start = ((bf16[32,32,1152]{2,1,0:T(8,128)(2,1)}), bf16[32,32,1152]{2,1,0:T(8,128)(2,1)S(1)}, u32[]{:S(2)}, u32[]{:S(2)}) async-start(bf16[32,32,1152]{2,1,0:T(8,128)(2,1)} %bitcast.14), calls=%async_computation | async-start | bytes 4718592 | tf_op jit(solution)/shard_map/all_to_all | solution.py:498
  22.4 1.1 tables.1
  23.4 27.5 %all-to-all-done.arrived_ref = bf16[32,32,1152]{2,1,0:T(8,128)(2,1)S(1)} async-done(((bf16[32,32,1152]{2,1,0:T(8,128)(2,1)}), bf16[32,32,1152]{2,1,0:T(8,128)(2,1)S(1)}, u32[]{:S(2)}, u32[]{:S(2)}) %all-to-all-start) | async-done | bytes 2359328 | tf_op jit(solution)/shard_map/all_to_all | solution.py:498
  50.9 5.2 %join.1 = (f32[32,128,128]{2,1,0:T(8,128)S(1)}, f32[32,128,128]{2,1,0:T(8,128)S(1)}) custom-call(s32[1,1]{1,0:T(1,128)} %bitcast.4.core_ref, s32[1,4]{1,0:T(1,128)S(1)} %copy-done.12, f32[1,4]{1,0:T(1,128)S(1)} %copy-done.13, s32[1,2]{1,0:T(1,128)S(1)} %copy-done.14, f32[1,2]{1,0:T(1,128)S(1)} %copy-done.15, s32[1,128]{1,0:T(1,128)S(1)} %copy-done.16, ...), custom_call_target="tpu_custom_call" | custom-call | flops 1342177280 | bytes 6291456 | tf_op jit(solution)/shard_map/join/pallas_call | solution.py:393
  56.2 1.3 copy-done.3
  57.5 1.4 copy-done.5
  58.9 20.5 %all-gather.2.cloned.1.call-done = bf16[256,32,128]{2,1,0:T(8,128)(2,1)} async-done(((bf16[32,32,128]{2,1,0:T(8,128)(2,1)}), bf16[256,32,128]{2,1,0:T(8,128)(2,1)}) %all-gather.2.cloned.1.call-update) | async-done | bytes 2097168 | tf_op jit(solution)/shard_map/all_gather | solution.py:492
  79.4 1.9 collective-permute-start.1
  81.3 1.6 copy-done
  83.0 3.4 %collective-permute-start = (bf16[128,32,128]{2,1,0:T(8,128)(2,1)S(1)}, bf16[128,32,128]{2,1,0:T(8,128)(2,1)S(1)}, u32[]{:S(2)}, u32[]{:S(2)}) collective-permute-start(bf16[128,32,128]{2,1,0:T(8,128)(2,1)S(1)} %pick.1), channel_id=1, source_target_pairs={{1,4},{5,8},{4,1},{9,12},{8,5},{13,16},{12,9},{17,20},{16,13},{21,... | collective-permute-start | bytes 3145736 | tf_op jit(solution)/shard_map/ppermute | solution.py:463
  86.4 1.6 copy-done.6
  87.9 7.5 %middle.3.inner_ref = bf16[128,32,128]{2,1,0:T(8,128)(2,1)S(1)} custom-call(s32[1]{0:T(128)} %bitcast.1.core_ref, bf16[32,96]{1,0:T(8,128)(2,1)S(1)} %get-tuple-element.31.az_ref, bf16[128,128]{1,0:T(8,128)(2,1)S(1)} %get-tuple-element.32.ay_ref, bf16[256,256]{1,0:T(8,128)(2,1)S(1)} %get-tuple-element.33.ax_ref, ...), custom_call_target="tpu_custom_call" | custom-call | flops 637534208 | bytes 6291456 | tf_op jit(solution)/shard_map/middle/pallas_call | solution.py:288
  95.4 3.0 %collective-permute-start.3 = (bf16[128,32,128]{2,1,0:T(8,128)(2,1)S(1)}, bf16[128,32,128]{2,1,0:T(8,128)(2,1)S(1)}, u32[]{:S(2)}, u32[]{:S(2)}) collective-permute-start(bf16[128,32,128]{2,1,0:T(8,128)(2,1)S(1)} %middle.3.inner_ref), channel_id=1, source_target_pairs={{0,1},{1,0},{2,3},{3,2},{4,5},{5,4},{6,7},{7,6},{8,9},{9,8},{10,11... | collective-permute-start | bytes 3145736 | tf_op jit(solution)/shard_map/ppermute | solution.py:453
  98.4 0.9 collective-permute-done
  99.3 7.5 %middle.2.outer_ref = bf16[128,32,128]{2,1,0:T(8,128)(2,1)S(1)} custom-call(s32[1]{0:T(128)} %bitcast.1.core_ref, bf16[32,96]{1,0:T(8,128)(2,1)S(1)} %get-tuple-element.31.az_ref, bf16[128,128]{1,0:T(8,128)(2,1)S(1)} %get-tuple-element.32.ay_ref, bf16[256,256]{1,0:T(8,128)(2,1)S(1)} %get-tuple-element.33.ax_ref, ...), custom_call_target="tpu_custom_call" | custom-call | flops 637534208 | bytes 6291456 | tf_op jit(solution)/shard_map/middle/pallas_call | solution.py:288
  106.8 4.5 %collective-permute-start.4 = (bf16[128,32,128]{2,1,0:T(8,128)(2,1)S(1)}, bf16[128,32,128]{2,1,0:T(8,128)(2,1)S(1)}, u32[]{:S(2)}, u32[]{:S(2)}) collective-permute-start(bf16[128,32,128]{2,1,0:T(8,128)(2,1)S(1)} %middle.2.outer_ref), channel_id=1, source_target_pairs={{0,1},{1,0},{2,3},{3,2},{4,5},{5,4},{6,7},{7,6},{8,9},{9,8},{10,11... | collective-permute-start | bytes 3145736 | tf_op jit(solution)/shard_map/ppermute | solution.py:453
  111.4 1.9 collective-permute-start.2
  113.6 13.9 %collective-permute-done.2.beside_ref = bf16[128,32,128]{2,1,0:T(8,128)(2,1)S(1)} collective-permute-done((bf16[128,32,128]{2,1,0:T(8,128)(2,1)S(1)}, bf16[128,32,128]{2,1,0:T(8,128)(2,1)S(1)}, u32[]{:S(2)}, u32[]{:S(2)}) %collective-permute-start.2) | collective-permute-done | bytes 1048608 | tf_op jit(solution)/shard_map/ppermute | solution.py:463
  127.5 4.5 %back.1 = f32[2,128,32,128]{3,2,1,0:T(8,128)} custom-call(s32[1]{0:T(128)} %bitcast.1.core_ref, bf16[32,96]{1,0:T(8,128)(2,1)S(1)} %get-tuple-element.30.table, bf16[128,32,128]{2,1,0:T(8,128)(2,1)S(1)} %collective-permute-done.2.beside_ref, bf16[128,32,128]{2,1,0:T(8,128)(2,1)S(1)} %middle.2.outer_ref, ...), custom_call_target="tpu_custom_call" | custom-call | flops 201326592 | bytes 9437184 | tf_op jit(solution)/shard_map/back/pallas_call | solution.py:429
  132.0 77.6 %reduce-scatter.2.cloned.1.call-done = f32[1,16,32,128]{3,2,1,0:T(8,128)} async-done(((f32[16,16,32,128]{3,2,1,0:T(8,128)}), f32[1,16,32,128]{3,2,1,0:T(8,128)}) %reduce-scatter.2.cloned.1.call-update) | async-done | bytes 262160 | tf_op jit(solution)/shard_map/reduce_scatter | solution.py:518
  209.6 1.8 finish.1
  (42 shorter events, 1.3 us)
Async XLA Ops:
  6.5 2.0 copy-start.18
  6.5 72.8 %all-gather.2.cloned.1.call-start = ((), (), s32[]{:S(2)}) async-start(), calls=%async_computation.2 | async-start | bytes 2359296 | tf_op jit(solution)/shard_map/all_gather | solution.py:492
  6.5 2.8 %copy-start.10 = (s32[1,512,1]{1,2,0:T(1,128)S(1)}, s32[1,512,1]{1,2,0:T(1,128)}, u32[]{:S(2)}) copy-start(s32[1,512,1]{1,2,0:T(1,128)} %param.15) | copy-start | bytes 6148
  6.5 2.8 %copy-start.11 = (s32[1,512]{1,0:T(1,128)S(1)}, s32[1,512]{1,0:T(1,128)}, u32[]{:S(2)}) copy-start(s32[1,512]{1,0:T(1,128)} %pos_ref.1) | copy-start | bytes 6148
  12.5 9.8 %copy-start.7 = (f32[1,64]{1,0:T(1,128)S(1)}, f32[1,64]{1,0:T(1,128)}, u32[]{:S(2)}) copy-start(f32[1,64]{1,0:T(1,128)} %psf_z_ref.1) | copy-start | bytes 772
  12.5 9.9 %copy-start.8 = (f32[1,16]{1,0:T(1,128)S(1)}, f32[1,16]{1,0:T(1,128)}, u32[]{:S(2)}) copy-start(f32[1,16]{1,0:T(1,128)} %psf_y_ref.1) | copy-start | bytes 196
  12.5 9.9 %copy-start.9 = (f32[1,16]{1,0:T(1,128)S(1)}, f32[1,16]{1,0:T(1,128)}, u32[]{:S(2)}) copy-start(f32[1,16]{1,0:T(1,128)} %psf_x_ref.1) | copy-start | bytes 196
  12.5 38.4 %copy-start.12 = (s32[1,4]{1,0:T(1,128)S(1)}, s32[1,4]{1,0:T(1,128)}, u32[]{:S(2)}) copy-start(s32[1,4]{1,0:T(1,128)} %off_z_ref.1) | copy-start | bytes 52
  12.5 38.4 %copy-start.13 = (f32[1,4]{1,0:T(1,128)S(1)}, f32[1,4]{1,0:T(1,128)}, u32[]{:S(2)}) copy-start(f32[1,4]{1,0:T(1,128)} %frac_z_ref.1) | copy-start | bytes 52
  12.5 38.4 %copy-start.14 = (s32[1,2]{1,0:T(1,128)S(1)}, s32[1,2]{1,0:T(1,128)}, u32[]{:S(2)}) copy-start(s32[1,2]{1,0:T(1,128)} %off_y_ref.1) | copy-start | bytes 28
  12.5 38.4 %copy-start.15 = (f32[1,2]{1,0:T(1,128)S(1)}, f32[1,2]{1,0:T(1,128)}, u32[]{:S(2)}) copy-start(f32[1,2]{1,0:T(1,128)} %frac_y_ref.1) | copy-start | bytes 28
  12.5 38.4 %copy-start.16 = (s32[1,128]{1,0:T(1,128)S(1)}, s32[1,128]{1,0:T(1,128)}, u32[]{:S(2)}) copy-start(s32[1,128]{1,0:T(1,128)} %off_x_ref.1) | copy-start | bytes 1540
  12.5 38.4 %copy-start.17 = (f32[1,128]{1,0:T(1,128)S(1)}, f32[1,128]{1,0:T(1,128)}, u32[]{:S(2)}) copy-start(f32[1,128]{1,0:T(1,128)} %frac_x_ref.1) | copy-start | bytes 1540
  12.6 38.3 %all-to-all-start = ((bf16[32,32,1152]{2,1,0:T(8,128)(2,1)}), bf16[32,32,1152]{2,1,0:T(8,128)(2,1)S(1)}, u32[]{:S(2)}, u32[]{:S(2)}) async-start(bf16[32,32,1152]{2,1,0:T(8,128)(2,1)} %bitcast.14), calls=%async_computation | async-start | bytes 4718592 | tf_op jit(solution)/shard_map/all_to_all | solution.py:498
  22.3 187.3 %reduce-scatter.2.cloned.1.call-start = ((), (), s32[]{:S(2)}) async-start(), calls=%async_computation.3 | async-start | bytes 4456448 | tf_op jit(solution)/shard_map/reduce_scatter | solution.py:518
  79.4 7.0 %collective-permute-start.1 = (bf16[2,128,32,128]{3,2,1,0:T(8,128)(2,1)}, bf16[2,128,32,128]{3,2,1,0:T(8,128)(2,1)S(1)}, u32[]{:S(2)}, u32[]{:S(2)}) collective-permute-start(bf16[2,128,32,128]{3,2,1,0:T(8,128)(2,1)} %bitcast.10), channel_id=1, source_target_pairs={{0,1},{1,0},{2,3},{3,2},{4,5},{5,4},{6,7},{7,6},{8,9},{9,8},{10,11... | collective-permute-start | bytes 6291464 | tf_op jit(solution)/shard_map/ppermute | solution.py:453
  81.3 1.6 copy-start
  82.9 3.5 %copy-start.1 = (bf16[256,32,128]{2,1,0:T(8,128)(2,1)S(1)}, bf16[256,32,128]{2,1,0:T(8,128)(2,1)}, u32[]{:S(2)}) copy-start(bf16[256,32,128]{2,1,0:T(8,128)(2,1)} %all-gather.2.cloned.1.call-done) | copy-start | bytes 6291460
  83.0 16.4 %copy-start.4 = (f32[32,128,128]{2,1,0:T(8,128)S(1)}, f32[32,128,128]{2,1,0:T(8,128)}, u32[]{:S(2)}) copy-start(f32[32,128,128]{2,1,0:T(8,128)} %copy-done.3) | copy-start | bytes 6291460
  83.0 16.4 %collective-permute-start = (bf16[128,32,128]{2,1,0:T(8,128)(2,1)S(1)}, bf16[128,32,128]{2,1,0:T(8,128)(2,1)S(1)}, u32[]{:S(2)}, u32[]{:S(2)}) collective-permute-start(bf16[128,32,128]{2,1,0:T(8,128)(2,1)S(1)} %pick.1), channel_id=1, source_target_pairs={{1,4},{5,8},{4,1},{9,12},{8,5},{13,16},{12,9},{17,20},{16,13},{21,... | collective-permute-start | bytes 3145736 | tf_op jit(solution)/shard_map/ppermute | solution.py:463
  86.4 1.6 copy-start.6
  95.4 17.9 %collective-permute-start.3 = (bf16[128,32,128]{2,1,0:T(8,128)(2,1)S(1)}, bf16[128,32,128]{2,1,0:T(8,128)(2,1)S(1)}, u32[]{:S(2)}, u32[]{:S(2)}) collective-permute-start(bf16[128,32,128]{2,1,0:T(8,128)(2,1)S(1)} %middle.3.inner_ref), channel_id=1, source_target_pairs={{0,1},{1,0},{2,3},{3,2},{4,5},{5,4},{6,7},{7,6},{8,9},{9,8},{10,11... | collective-permute-start | bytes 3145736 | tf_op jit(solution)/shard_map/ppermute | solution.py:453
  106.8 6.8 %collective-permute-start.4 = (bf16[128,32,128]{2,1,0:T(8,128)(2,1)S(1)}, bf16[128,32,128]{2,1,0:T(8,128)(2,1)S(1)}, u32[]{:S(2)}, u32[]{:S(2)}) collective-permute-start(bf16[128,32,128]{2,1,0:T(8,128)(2,1)S(1)} %middle.2.outer_ref), channel_id=1, source_target_pairs={{0,1},{1,0},{2,3},{3,2},{4,5},{5,4},{6,7},{7,6},{8,9},{9,8},{10,11... | collective-permute-start | bytes 3145736 | tf_op jit(solution)/shard_map/ppermute | solution.py:453
  111.4 16.1 %collective-permute-start.2 = (bf16[128,32,128]{2,1,0:T(8,128)(2,1)S(1)}, bf16[128,32,128]{2,1,0:T(8,128)(2,1)S(1)}, u32[]{:S(2)}, u32[]{:S(2)}) collective-permute-start(bf16[128,32,128]{2,1,0:T(8,128)(2,1)S(1)} %middle.2.outer_ref), channel_id=1, source_target_pairs={{1,4},{5,8},{4,1},{9,12},{8,5},{13,16},{12,9},{17,20},{16,13},{21,... | collective-permute-start | bytes 3145736 | tf_op jit(solution)/shard_map/ppermute | solution.py:463
  (3 other events, 4.1 us)
Sparse Core Ops, SparseCore 0:
  9.4 69.9 all-gather.1
  132.1 77.4 reduce-scatter.1
